TPU v7x, 32 devices: a whole 2x2x4 slice. The times are simulated.
32 devices in a mesh: dom: 8 (over z, y), case: 4 (over x, core).
Axes of the slice: x: 2, y: 2, z: 4, core: 2. Of those that a mesh axis runs over, the one named last changes fastest.
Arguments:
- dual_ops: float32 [16, 1536, 1536], P('dom')
- modes: bfloat16 [16, 16, 1536], P('dom'), may hold values from -0.15625 to 0.15625
- coarse_rows: float32 [16, 8, 16, 16], P('dom'), may hold values from -1 to 1
- coarse_cols: int32 [16, 8], P('dom'), may hold values from 0 to 15, as said below
- row_perm: int32 [16, 1536], P('dom'), may hold values from 0 to 1535, each once within a row
- iface_size: int32 [16], P('dom'), may hold values from 256 to 768, as said below
- rhs: float32 [16, 768, 512], P('dom', None, 'case'), may hold values from -6 to 6
Outputs:
- solution: float32 [16, 768, 512], P('dom', None, 'case')
- residual: float32 [16, 768, 512], P('dom', None, 'case')
- history: float32 [4, 512], P(None, 'case')
- peak_norm: float32 [4], replicated
Inputs may be any that keep to these rules, and one draw needn't show every extreme that they name: `iface_size`: interfaces carry between 256 and 768 multipliers; both ends are reached in every draw. `coarse_cols`: for every subdomain s the first three entries are s, (s - 1) mod 16 and (s + 1) mod 16; the others are any subdomains, repeats allowed. `row_perm`: each row is a permutation of the local rows.
All inputs are finite; a program needn't handle non-finite values.
Results may differ from a plain program's by a relative error of at most 0.0056.
Values may be sent and summed in bfloat16 or wider, within the bound.
A program may use at most 192 MiB of HBM per device.

v0:
```python
import jax
import jax.numpy as jnp
from jax import lax
from jax.sharding import PartitionSpec as P

STEPS = 4


low_bound = 2.0
high_bound = 14.0
epsilon = 1e-06
highest = lax.Precision.HIGHEST


def from_behind(block, axis, distance):
    devices = range(lax.axis_size(axis))
    route = [((i - distance) % len(devices), i) for i in devices]
    return lax.ppermute(block, axis, route)


def slot_form(left_side, right_side):
    return jnp.concatenate([-left_side, right_side], axis=1)


def shards(dual_ops, modes, coarse_rows, coarse_cols, row_perm, iface_size, rhs):
    sub_count, half_width, case_count = rhs.shape
    dom_count = lax.axis_size("dom") * sub_count
    live_mask = (
        lax.broadcasted_iota(jnp.int32, (sub_count, half_width), 1) < iface_size[:, None]
    ).astype(jnp.float32)[:, :, None]
    slot_ops = jax.vmap(lambda matrix, ordering: matrix[ordering].T[ordering])(dual_ops, row_perm)
    slot_modes_low = jax.vmap(lambda block_rows, ordering: block_rows[:, ordering])(modes, row_perm)
    slot_modes = slot_modes_low.astype(jnp.float32)
    int_pack = jnp.concatenate([coarse_cols, iface_size[:, None]], axis=1)
    prior_ints = from_behind(int_pack[-1], "dom", 1)
    next_ints = from_behind(int_pack[0], "dom", -1)
    prior_modes = from_behind(slot_modes_low[-1], "dom", 1)
    next_modes = from_behind(slot_modes_low[0], "dom", -1)
    prior_blocks = from_behind(coarse_rows[-1], "dom", 1)
    next_blocks = from_behind(coarse_rows[0], "dom", -1)
    ext_ints = jnp.concatenate([prior_ints[None], int_pack, next_ints[None]], axis=0)
    block_count = coarse_cols.shape[1]
    ext_cols = ext_ints[:, :block_count]
    ext_size = ext_ints[:, block_count]
    ext_modes = jnp.concatenate(
        [prior_modes[None], slot_modes_low, next_modes[None]], axis=0
    ).astype(jnp.float32)
    ext_blocks = jnp.concatenate([prior_blocks[None], coarse_rows, next_blocks[None]], axis=0)
    ext_live = (
        lax.broadcasted_iota(jnp.int32, (sub_count + 2, half_width), 1) < ext_size[:, None]
    ).astype(jnp.float32)[:, :, None]

    def build_local(vector):
        prior_rim = from_behind(vector[-1], "dom", 1)
        left_side = jnp.concatenate([prior_rim[None], vector[:-1]], axis=0)
        return slot_form(left_side, vector)

    def select_columns(columns, all_coefficients):
        table = (
            columns[:, :, None] == lax.broadcasted_iota(jnp.int32, (1, 1, dom_count), 2)
        ).astype(jnp.float32)
        return jnp.einsum(
            "sqd,djc->sqjc", table, all_coefficients.astype(jnp.float32), precision=highest
        )

    def gather_coefficients(slot_rows):
        coefficients = jnp.einsum("sjn,snc->sjc", slot_modes, slot_rows, precision=highest).astype(
            jnp.bfloat16
        )
        return lax.all_gather(coefficients, "dom", axis=0, tiled=True)

    centre = 0.5 * (high_bound + low_bound)
    radius = 0.5 * (high_bound - low_bound)
    spread_ratio = centre / radius
    ratio_now = 1.0 / spread_ratio
    start_vector = rhs * live_mask
    picked = select_columns(coarse_cols, gather_coefficients(build_local(start_vector)))
    amounts = jnp.einsum("sqij,sqjc->sic", coarse_rows, picked, precision=highest)
    slot_rows = jnp.einsum("sjn,sjc->snc", slot_modes, amounts, precision=highest)
    lower_half = slot_rows[:, :half_width]
    upper_half = slot_rows[:, half_width:]
    later_rim = from_behind(lower_half[0], "dom", -1)
    following = jnp.concatenate([lower_half[1:], later_rim[None]], axis=0)
    residual = start_vector - (upper_half - following) * live_mask
    direction = residual / centre
    local_residual = build_local(residual)
    local_direction = local_residual / centre
    solution = jnp.zeros_like(rhs)
    norm_list = []
    for turn_index in range(STEPS):
        solution = solution + direction
        product = jnp.einsum("smn,smc->snc", slot_ops, local_direction, precision=highest)
        local_lower_half = product[:, :half_width]
        local_upper_half = product[:, half_width:]
        prior_upper = from_behind(local_upper_half[-1], "dom", 1)
        later_lower = from_behind(local_lower_half[0], "dom", -1)
        local_following = jnp.concatenate([local_lower_half[1:], later_lower[None]], axis=0)
        mapped = (local_upper_half - local_following) * live_mask
        first_value = (prior_upper - local_lower_half[0]) * ext_live[0]
        local_left_side = jnp.concatenate([first_value[None], mapped[:-1]], axis=0)
        mapped, local_mapped = (mapped, slot_form(local_left_side, mapped))
        wide_picked = select_columns(ext_cols, gather_coefficients(local_mapped))
        wide_amounts = jnp.einsum("sqij,sqjc->sic", ext_blocks, wide_picked, precision=highest)
        spread = jnp.einsum("sjn,sjc->snc", ext_modes, wide_amounts, precision=highest)
        lower_part = spread[:, :half_width]
        upper_part = spread[:, half_width:]
        joined = (upper_part[:-1] - lower_part[1:]) * ext_live[:-1]
        correction = joined[1:]
        local_correction = slot_form(joined[:-1], joined[1:])
        residual = residual - (mapped - correction)
        local_residual = local_residual - (local_mapped - local_correction)
        partial_value = jnp.sum(residual * residual, axis=(0, 1))
        norm_list.append(jnp.sqrt(lax.psum(partial_value, "dom") + epsilon))
        if turn_index + 1 < STEPS:
            ratio_next = 1.0 / (2.0 * spread_ratio - ratio_now)
            direction = ratio_next * ratio_now * direction + 2.0 * ratio_next / radius * residual
            local_direction = (
                ratio_next * ratio_now * local_direction
                + 2.0 * ratio_next / radius * local_residual
            )
            ratio_now = ratio_next
    history = jnp.stack(norm_list)
    peak_norm = lax.pmax(jnp.max(history, axis=1), "case")
    return (solution, residual, history, peak_norm)


def solution(mesh):
    in_specs = (
        P("dom", None, None),
        P("dom", None, None),
        P("dom", None, None, None),
        P("dom", None),
        P("dom", None),
        P("dom"),
        P("dom", None, "case"),
    )
    out_specs = (P("dom", None, "case"), P("dom", None, "case"), P(None, "case"), P())
    return jax.shard_map(shards, mesh=mesh, in_specs=in_specs, out_specs=out_specs, check_vma=False)
```

profile of v0, /device:TPU:0, one launch (start us, length us, event | category | flops | bytes accessed | tf_op | source)
XLA Modules:
  0.0 602.8 jit_solution(7699816429259120163)
XLA Ops:
  3.6 3.0 collective-permute-start
  7.3 16.5 %gather_fusion = bf16[3072,16]{1,0:T(8,128)(2,1)S(1)} fusion(bf16[2,16,1536]{1,2,0:T(8,128)(2,1)S(1)} %copy.28, s32[3072]{0:T(1024)S(1)} %reshape.35), kind=kCustom, calls=%fused_computation | custom fusion | bytes 221184 | tf_op jit(solution)/shard_map/vmap()/gather | solution.py:32
  24.8 30.9 %all_gather.15 = bf16[16,16,128]{2,1,0:T(8,128)(2,1)S(1)} all-gather(bf16[2,16,128]{2,1,0:T(8,128)(2,1)S(1)} %fusion.33), channel_id=1, replica_groups=mesh['dom'=8,'case'=4] {'dom'}, dimensions={0}, use_global_device_ids=true | all-gather | bytes 73728 | tf_op jit(solution)/shard_map/all_gather | solution.py:70
  57.9 2.7 collective-permute-start.1
  60.6 2.0 collective-permute-start.8
  63.2 2.7 collective-permute-start.7
  66.2 68.1 %gather_fusion.1 = f32[3072,1536]{1,0:T(8,128)} fusion(f32[2,1536,1536]{2,1,0:T(8,128)} %param.7, s32[3072]{0:T(1024)S(1)} %reshape.35), kind=kCustom, calls=%fused_computation.1 | custom fusion | bytes 37773312 | tf_op jit(solution)/shard_map/vmap()/gather | solution.py:31
  134.3 18.7 %copy.34 = f32[2,1536,1536]{1,2,0:T(8,128)} copy(f32[2,1536,1536]{2,1,0:T(8,128)} %bitcast.153) | data formatting | bytes 37748736 | tf_op jit(solution)/shard_map/vmap()/gather | solution.py:31
  153.0 68.1 %gather_fusion.2 = f32[3072,1536]{1,0:T(8,128)} fusion(f32[2,1536,1536]{2,1,0:T(8,128)} %bitcast.146, s32[3072]{0:T(1024)S(1)} %reshape.35), kind=kCustom, calls=%fused_computation.2 | custom fusion | bytes 37773312 | tf_op jit(solution)/shard_map/vmap()/gather | solution.py:31
  224.1 4.6 collective-permute-start.5
  228.8 5.2 collective-permute-done.2
  234.1 32.9 %fusion.18 = f32[2,1536,128]{2,1,0:T(8,128)S(1)} fusion(f32[2,1536,1536]{2,1,0:T(8,128)} %bitcast.147, f32[2,768,128]{2,1,0:T(8,128)S(1)} %fusion.44, f32[2,768,128]{2,1,0:T(8,128)S(1)} %maximum_negate_fusion.1), kind=kOutput, calls=%fused_computation.29 | convolution fusion | flops 7248543744 | bytes 22020096 | tf_op jit(solution)/shard_map/smn,smc->snc/dot_general | solution.py:92
  267.1 2.6 collective-permute-start.3
  270.0 5.5 collective-permute-done.3
  275.9 4.6 collective-permute-done.10
  281.7 30.7 %all_gather.16 = bf16[16,16,128]{2,1,0:T(8,128)(2,1)S(1)} all-gather(bf16[2,16,128]{2,1,0:T(8,128)(2,1)S(1)} %fusion.27), channel_id=1, replica_groups=mesh['dom'=8,'case'=4] {'dom'}, dimensions={0}, use_global_device_ids=true | all-gather | bytes 73728 | tf_op jit(solution)/shard_map/all_gather | solution.py:70
  317.5 41.9 %fusion.115 = f32[2,1536,128]{2,1,0:T(8,128)S(1)} fusion(f32[2,1536,1536]{2,1,0:T(8,128)S(1)} %bitcast.150, f32[2,1536,128]{2,1,0:T(8,128)S(1)} %multiply_add_fusion.1), kind=kOutput, calls=%fused_computation.185 | convolution fusion | flops 7247757312 | bytes 22020096 | tf_op jit(solution)/shard_map/smn,smc->snc/dot_general | solution.py:92
  361.6 5.8 collective-permute-done.11
  367.8 3.9 collective-permute-done.12
  372.9 30.5 %all_gather.17 = bf16[16,16,128]{2,1,0:T(8,128)(2,1)S(1)} all-gather(bf16[2,16,128]{2,1,0:T(8,128)(2,1)S(1)} %fusion.28), channel_id=1, replica_groups=mesh['dom'=8,'case'=4] {'dom'}, dimensions={0}, use_global_device_ids=true | all-gather | bytes 73728 | tf_op jit(solution)/shard_map/all_gather | solution.py:70
  409.9 33.2 %fusion.20 = f32[2,1536,128]{2,1,0:T(8,128)} fusion(f32[2,1536,1536]{2,1,0:T(8,128)S(1)} %bitcast.151, f32[2,1536,128]{2,1,0:T(8,128)} %fusion.5, f32[2,1536,128]{2,1,0:T(8,128)S(1)} %multiply_add_fusion.1), kind=kOutput, calls=%fused_computation.31 | convolution fusion | flops 7248936960 | bytes 23592960 | tf_op jit(solution)/shard_map/smn,smc->snc/dot_general | solution.py:92
  444.6 2.1 collective-permute-start.13
  446.6 5.8 collective-permute-done.13
  452.9 4.3 collective-permute-done.14
  458.4 30.5 %all_gather.18 = bf16[16,16,128]{2,1,0:T(8,128)(2,1)S(1)} all-gather(bf16[2,16,128]{2,1,0:T(8,128)(2,1)S(1)} %fusion.29), channel_id=1, replica_groups=mesh['dom'=8,'case'=4] {'dom'}, dimensions={0}, use_global_device_ids=true | all-gather | bytes 73728 | tf_op jit(solution)/shard_map/all_gather | solution.py:70
  494.4 32.6 %fusion.9 = f32[2,1536,128]{2,1,0:T(8,128)S(1)} fusion(f32[2,1536,1536]{2,1,0:T(8,128)S(1)} %bitcast.152, f32[2,1536,128]{2,1,0:T(8,128)S(1)} %copy-done, f32[2,768,128]{2,1,0:T(8,128)} %get-tuple-element.35, f32[2,768,128]{2,1,0:T(8,128)} %get-tuple-element.34, f32[2,1536,128]{2,1,0:T(8,128)S(1)} %multiply_add_fusion.1, f32[2,768,128]{2,1,0:T(8,128)S(1)} %fusion.40, ...), kind=kOutput, calls=%fused_computation.19 | convolution fusion | flops 7251689472 | bytes 26738688 | tf_op jit(solution)/shard_map/smn,smc->snc/dot_general | solution.py:92
  527.1 1.8 collective-permute-start.15
  529.1 5.8 collective-permute-done.15
  535.4 4.0 collective-permute-done.16
  540.5 30.5 %all_gather.19 = bf16[16,16,128]{2,1,0:T(8,128)(2,1)S(1)} all-gather(bf16[2,16,128]{2,1,0:T(8,128)(2,1)S(1)} %fusion.30), channel_id=1, replica_groups=mesh['dom'=8,'case'=4] {'dom'}, dimensions={0}, use_global_device_ids=true | all-gather | bytes 73728 | tf_op jit(solution)/shard_map/all_gather | solution.py:70
  576.6 19.1 %all-reduce = (f32[128]{0:T(128)S(1)}, f32[128]{0:T(128)S(1)}, f32[128]{0:T(128)S(1)}, f32[128]{0:T(128)S(1)}) all-reduce(f32[128]{0:T(128)S(1)} %get-tuple-element.16, f32[128]{0:T(128)S(1)} %get-tuple-element.14, f32[128]{0:T(128)S(1)} %get-tuple-element.12, f32[128]{0:T(128)S(1)} %get-tuple-element.10), channel_id=1, replica_groups=mesh['dom'=8,'case'=4] {'dom'}, use_global_device_ids=true, to_apply=%region_7.0 | all-reduce | flops 512 | bytes 4096 | tf_op jit(solution)/shard_map/psum | solution.py:113
  596.4 6.2 %pmax.7 = f32[4]{0:T(128)} all-reduce(f32[4]{0:T(128)S(1)} %get-tuple-element.8), channel_id=1, replica_groups=mesh['dom'=8,'case'=4] {'case'}, use_global_device_ids=true, to_apply=%region_9.0 | all-reduce | flops 4 | bytes 32 | tf_op jit(solution)/shard_map/pmax | solution.py:123
  (134 shorter events, 44.7 us)
Async XLA Ops:
  1.4 5.3 copy-start.11
  2.8 4.2 copy-start.12
  2.8 4.3 copy-start.8
  2.8 4.4 copy-start.14
  3.6 20.2 %collective-permute-start = (f32[768,128]{1,0:T(8,128)}, f32[768,128]{1,0:T(8,128)S(1)}, u32[]{:S(2)}, u32[]{:S(2)}) collective-permute-start(f32[768,128]{1,0:T(8,128)} %get-tuple-element.43), channel_id=1, source_target_pairs={{28,0},{0,4},{4,8},{8,12},{12,16},{16,20},{20,24},{24,28},{29,1},{... | collective-permute-start | bytes 1179656 | tf_op jit(solution)/shard_map/ppermute | solution.py:18
  7.0 16.8 %copy-start.13 = (s32[2,8]{1,0:T(2,128)S(1)}, s32[2,8]{1,0:T(2,128)}, u32[]{:S(2)}) copy-start(s32[2,8]{1,0:T(2,128)} %param.10) | copy-start | bytes 196
  57.9 163.1 %collective-permute-start.1 = (f32[768,128]{1,0:T(8,128)S(1)}, f32[768,128]{1,0:T(8,128)S(1)}, u32[]{:S(2)}, u32[]{:S(2)}) collective-permute-start(f32[768,128]{1,0:T(8,128)S(1)} %get-tuple-element.33), channel_id=1, source_target_pairs={{4,0},{8,4},{12,8},{16,12},{20,16},{24,20},{28,24},{0,28},{5,1},{9... | collective-permute-start | bytes 1179656 | tf_op jit(solution)/shard_map/ppermute | solution.py:18
  60.5 163.5 %collective-permute-start.9 = (s32[9]{0:T(128)S(1)}, s32[9]{0:T(128)S(1)}, u32[]{:S(2)}, u32[]{:S(2)}) collective-permute-start(s32[9]{0:T(128)S(1)} %get-tuple-element.50), channel_id=1, source_target_pairs={{4,0},{8,4},{12,8},{16,12},{20,16},{24,20},{28,24},{0,28},{5,1},{9... | collective-permute-start | bytes 116 | tf_op jit(solution)/shard_map/ppermute | solution.py:18
  60.6 168.2 %collective-permute-start.8 = (s32[9]{0:T(128)S(1)}, s32[9]{0:T(128)S(1)}, u32[]{:S(2)}, u32[]{:S(2)}) collective-permute-start(s32[9]{0:T(128)S(1)} %get-tuple-element.49), channel_id=1, source_target_pairs={{28,0},{0,4},{4,8},{8,12},{12,16},{16,20},{20,24},{24,28},{29,1},{... | collective-permute-start | bytes 116 | tf_op jit(solution)/shard_map/ppermute | solution.py:18
  63.2 249.3 %collective-permute-start.7 = (f32[8,16,16]{2,1,0:T(8,128)}, f32[8,16,16]{2,1,0:T(8,128)S(1)}, u32[]{:S(2)}, u32[]{:S(2)}) collective-permute-start(f32[8,16,16]{2,1,0:T(8,128)} %get-tuple-element.46), channel_id=1, source_target_pairs={{4,0},{8,4},{12,8},{16,12},{20,16},{24,20},{28,24},{0,28},{5,1},{9... | collective-permute-start | bytes 24584 | tf_op jit(solution)/shard_map/ppermute | solution.py:18
  66.0 246.6 %collective-permute-start.6 = (f32[8,16,16]{2,1,0:T(8,128)}, f32[8,16,16]{2,1,0:T(8,128)S(1)}, u32[]{:S(2)}, u32[]{:S(2)}) collective-permute-start(f32[8,16,16]{2,1,0:T(8,128)} %get-tuple-element.45), channel_id=1, source_target_pairs={{28,0},{0,4},{4,8},{8,12},{12,16},{16,20},{20,24},{24,28},{29,1},{... | collective-permute-start | bytes 24584 | tf_op jit(solution)/shard_map/ppermute | solution.py:18
  223.5 10.5 %collective-permute-start.2 = (f32[768,128]{1,0:T(8,128)S(1)}, f32[768,128]{1,0:T(8,128)S(1)}, u32[]{:S(2)}, u32[]{:S(2)}) collective-permute-start(f32[768,128]{1,0:T(8,128)S(1)} %get-tuple-element.41), channel_id=1, source_target_pairs={{28,0},{0,4},{4,8},{8,12},{12,16},{16,20},{20,24},{24,28},{29,1},{... | collective-permute-start | bytes 1179656 | tf_op jit(solution)/shard_map/ppermute | solution.py:18
  224.1 89.2 %collective-permute-start.5 = (bf16[16,1536]{1,0:T(8,128)(2,1)S(1)}, bf16[16,1536]{1,0:T(8,128)(2,1)S(1)}, u32[]{:S(2)}, u32[]{:S(2)}) collective-permute-start(bf16[16,1536]{1,0:T(8,128)(2,1)S(1)} %get-tuple-element.48), channel_id=1, source_target_pairs={{4,0},{8,4},{12,8},{16,12},{20,16},{24,20},{28,24},{0,28},{5,1},{9... | collective-permute-start | bytes 147464 | tf_op jit(solution)/shard_map/ppermute | solution.py:18
  234.1 83.4 %slice-start = ((s8[18874368]{0:T(1024)(128)(4,1)}), s8[4194304]{0:T(1024)(128)(4,1)S(1)}, s32[]{:S(2)}) async-start(s8[18874368]{0:T(1024)(128)(4,1)} %bitcast.148), calls=%async_computation | async-start | bytes 8388608
  234.1 83.4 %slice-start.1 = ((s8[18874368]{0:T(1024)(128)(4,1)}), s8[4194304]{0:T(1024)(128)(4,1)S(1)}, s32[]{:S(2)}) async-start(s8[18874368]{0:T(1024)(128)(4,1)} %bitcast.148), calls=%async_computation.1 | async-start | bytes 8388608
  234.1 83.4 %slice-start.2 = ((s8[18874368]{0:T(1024)(128)(4,1)}), s8[4194304]{0:T(1024)(128)(4,1)S(1)}, s32[]{:S(2)}) async-start(s8[18874368]{0:T(1024)(128)(4,1)} %bitcast.148), calls=%async_computation.2 | async-start | bytes 8388608
  267.1 8.4 %collective-permute-start.3 = (f32[768,128]{1,0:T(8,128)S(1)}, f32[768,128]{1,0:T(8,128)S(1)}, u32[]{:S(2)}, u32[]{:S(2)}) collective-permute-start(f32[768,128]{1,0:T(8,128)S(1)} %get-tuple-element.30), channel_id=1, source_target_pairs={{4,0},{8,4},{12,8},{16,12},{20,16},{24,20},{28,24},{0,28},{5,1},{9... | collective-permute-start | bytes 1179656 | tf_op jit(solution)/shard_map/ppermute | solution.py:18
  269.9 10.6 %collective-permute-start.10 = (f32[768,128]{1,0:T(8,128)S(1)}, f32[768,128]{1,0:T(8,128)S(1)}, u32[]{:S(2)}, u32[]{:S(2)}) collective-permute-start(f32[768,128]{1,0:T(8,128)S(1)} %get-tuple-element.29), channel_id=1, source_target_pairs={{28,0},{0,4},{4,8},{8,12},{12,16},{16,20},{20,24},{24,28},{29,1},{... | collective-permute-start | bytes 1179656 | tf_op jit(solution)/shard_map/ppermute | solution.py:18
  275.5 37.8 %collective-permute-start.4 = (bf16[16,1536]{1,0:T(8,128)(2,1)S(1)}, bf16[16,1536]{1,0:T(8,128)(2,1)S(1)}, u32[]{:S(2)}, u32[]{:S(2)}) collective-permute-start(bf16[16,1536]{1,0:T(8,128)(2,1)S(1)} %get-tuple-element.47), channel_id=1, source_target_pairs={{28,0},{0,4},{4,8},{8,12},{12,16},{16,20},{20,24},{24,28},{29,1},{... | collective-permute-start | bytes 147464 | tf_op jit(solution)/shard_map/ppermute | solution.py:18
  280.8 36.7 %slice-start.3 = ((s8[18874368]{0:T(1024)(128)(4,1)}), s8[4194304]{0:T(1024)(128)(4,1)S(1)}, s32[]{:S(2)}) async-start(s8[18874368]{0:T(1024)(128)(4,1)} %bitcast.148), calls=%async_computation.3 | async-start | bytes 8388608
  315.2 2.2 slice-start.4
  359.5 7.9 %collective-permute-start.11 = (f32[768,128]{1,0:T(8,128)S(1)}, f32[768,128]{1,0:T(8,128)S(1)}, u32[]{:S(2)}, u32[]{:S(2)}) collective-permute-start(f32[768,128]{1,0:T(8,128)S(1)} %get-tuple-element.27), channel_id=1, source_target_pairs={{4,0},{8,4},{12,8},{16,12},{20,16},{24,20},{28,24},{0,28},{5,1},{9... | collective-permute-start | bytes 1179656 | tf_op jit(solution)/shard_map/ppermute | solution.py:18
  361.1 10.6 %collective-permute-start.12 = (f32[768,128]{1,0:T(8,128)S(1)}, f32[768,128]{1,0:T(8,128)S(1)}, u32[]{:S(2)}, u32[]{:S(2)}) collective-permute-start(f32[768,128]{1,0:T(8,128)S(1)} %get-tuple-element.26), channel_id=1, source_target_pairs={{28,0},{0,4},{4,8},{8,12},{12,16},{16,20},{20,24},{24,28},{29,1},{... | collective-permute-start | bytes 1179656 | tf_op jit(solution)/shard_map/ppermute | solution.py:18
  407.1 1.3 copy-start.3
  443.1 9.4 %copy-start.1 = (f32[2,1536,128]{2,1,0:T(8,128)S(1)}, f32[2,1536,128]{2,1,0:T(8,128)}, u32[]{:S(2)}) copy-start(f32[2,1536,128]{2,1,0:T(8,128)} %fusion.20) | copy-start | bytes 4718596
  444.6 7.9 %collective-permute-start.13 = (f32[768,128]{1,0:T(8,128)S(1)}, f32[768,128]{1,0:T(8,128)S(1)}, u32[]{:S(2)}, u32[]{:S(2)}) collective-permute-start(f32[768,128]{1,0:T(8,128)S(1)} %get-tuple-element.24), channel_id=1, source_target_pairs={{4,0},{8,4},{12,8},{16,12},{20,16},{24,20},{28,24},{0,28},{5,1},{9... | collective-permute-start | bytes 1179656 | tf_op jit(solution)/shard_map/ppermute | solution.py:18
  446.6 10.6 %collective-permute-start.14 = (f32[768,128]{1,0:T(8,128)S(1)}, f32[768,128]{1,0:T(8,128)S(1)}, u32[]{:S(2)}, u32[]{:S(2)}) collective-permute-start(f32[768,128]{1,0:T(8,128)S(1)} %get-tuple-element.23), channel_id=1, source_target_pairs={{28,0},{0,4},{4,8},{8,12},{12,16},{16,20},{20,24},{24,28},{29,1},{... | collective-permute-start | bytes 1179656 | tf_op jit(solution)/shard_map/ppermute | solution.py:18
  457.5 32.4 %copy-start.7 = (f32[2,768,128]{2,1,0:T(8,128)}, f32[2,768,128]{2,1,0:T(8,128)S(1)}, u32[]{:S(2)}) copy-start(f32[2,768,128]{2,1,0:T(8,128)S(1)} %maximum_negate_fusion.4) | copy-start | bytes 2359300
  492.6 1.8 copy-start
  527.1 7.9 %collective-permute-start.15 = (f32[768,128]{1,0:T(8,128)S(1)}, f32[768,128]{1,0:T(8,128)S(1)}, u32[]{:S(2)}, u32[]{:S(2)}) collective-permute-start(f32[768,128]{1,0:T(8,128)S(1)} %get-tuple-element.21), channel_id=1, source_target_pairs={{4,0},{8,4},{12,8},{16,12},{20,16},{24,20},{28,24},{0,28},{5,1},{9... | collective-permute-start | bytes 1179656 | tf_op jit(solution)/shard_map/ppermute | solution.py:18
  528.8 10.5 %collective-permute-start.16 = (f32[768,128]{1,0:T(8,128)S(1)}, f32[768,128]{1,0:T(8,128)S(1)}, u32[]{:S(2)}, u32[]{:S(2)}) collective-permute-start(f32[768,128]{1,0:T(8,128)S(1)} %get-tuple-element.20), channel_id=1, source_target_pairs={{28,0},{0,4},{4,8},{8,12},{12,16},{16,20},{20,24},{24,28},{29,1},{... | collective-permute-start | bytes 1179656 | tf_op jit(solution)/shard_map/ppermute | solution.py:18
  573.6 1.4 copy-start.9
  (5 other events, 5.0 us)
where the time goes:
time: 606 us; the launch traced here: 603 us
  local copies, waits for them, and re-layouts  181 us (30%)
  blocking collectives  178 us (29%)
  matrix products  156 us (26%)
  waiting for transfers between devices  44.9 us (7%)
  starting transfers between devices  24.5 us (4%)
  other arithmetic  16.3 us (3%)
    gather x3, local copies, waits for them, and re-layouts, shards(): matrix[ordering].T[ordering]  155 us
    all_gather x5, blocking collectives, gather_coefficients(): return lax.all_gather(coefficients, 'dom', axis=0, tiled=True)  153 us
    dot_general x4, matrix products, shards(): jnp.einsum('smn,smc->snc', slot_ops, local_direction, precision=highest)  141 us
    ppermute x17, waiting for transfers between devices, from_behind(): return lax.ppermute(block, axis, route)  44.9 us
    ppermute x17, starting transfers between devices, from_behind(): return lax.ppermute(block, axis, route)  24.5 us
    psum x1, blocking collectives, shards(): norm_list.append(jnp.sqrt(lax.psum(partial_value, 'dom') + epsilon))  19.1 us
    gather x3, local copies, waits for them, and re-layouts, shards(): block_rows[:, ordering]  16.7 us
  transfers between devices with their start and end apart: 17, of which 9 were waited for; matrix products, arithmetic and copies ran while one was open for 35% of the time, Pallas kernels for 0%

commit v1 on v0

v1 whole, which is shorter than its diff:
```python
import functools

import jax
import jax.numpy as jnp
from jax import lax
from jax.experimental import pallas as pl
from jax.experimental.pallas import tpu as pltpu
from jax.sharding import PartitionSpec as P

STEPS = 4


low_bound = 2.0
high_bound = 14.0
epsilon = 1e-06
highest = lax.Precision.HIGHEST
f32, bf16 = jnp.float32, jnp.bfloat16


def from_behind(block, axis, distance):
    devices = range(lax.axis_size(axis))
    route = [((i - distance) % len(devices), i) for i in devices]
    return lax.ppermute(block, axis, route)


def gather_kernel(axes, sizes, x_ref, out_ref, own_sem, send_sem, recv_sem):
    me = [lax.axis_index(axis) for axis in axes]

    def flat(position):
        index = 0
        for at, size in zip(position, sizes):
            index = index * size + at
        return index

    offsets = [()]
    for size in sizes:
        offsets = [o + (k,) for o in offsets for k in range(size)]
    targets = [
        {axis: lax.rem(at + k, size) for axis, at, k, size in zip(axes, me, offset, sizes)}
        for offset in offsets[1:]
    ]
    barrier = pltpu.get_barrier_semaphore()
    for target in targets:
        pl.semaphore_signal(
            barrier, inc=1, device_id=target, device_id_type=pl.DeviceIdType.MESH
        )
    own = pltpu.make_async_copy(x_ref, out_ref.at[flat(me)], own_sem)
    own.start()
    pl.semaphore_wait(barrier, len(targets))
    copies = []
    for k, target in enumerate(targets):
        copy = pltpu.make_async_remote_copy(
            src_ref=x_ref,
            dst_ref=out_ref.at[flat(me)],
            send_sem=send_sem.at[k],
            recv_sem=recv_sem.at[k],
            device_id=target,
            device_id_type=pl.DeviceIdType.MESH,
        )
        copy.start()
        copies.append(copy)
    own.wait()
    for copy in copies:
        copy.wait()


def push_gather(block, axes, collective_id):
    sizes = tuple(lax.axis_size(axis) for axis in axes)
    count = 1
    for size in sizes:
        count *= size
    return pl.pallas_call(
        functools.partial(gather_kernel, axes, sizes),
        out_shape=jax.ShapeDtypeStruct((count,) + block.shape, block.dtype),
        in_specs=[pl.BlockSpec(memory_space=pltpu.VMEM)],
        out_specs=pl.BlockSpec(memory_space=pltpu.VMEM),
        scratch_shapes=[
            pltpu.SemaphoreType.DMA,
            pltpu.SemaphoreType.DMA((count - 1,)),
            pltpu.SemaphoreType.DMA((count - 1,)),
        ],
        compiler_params=pltpu.CompilerParams(collective_id=collective_id, has_side_effects=True),
    )(block)


def put_split(ref, rows, value):
    width = value.shape[1]
    high = value.astype(bf16)
    ref[rows, :width] = high
    ref[rows, width:] = (value - high.astype(f32)).astype(bf16)


def joined_halves(pair):
    width = pair.shape[1] // 2
    return pair[:, :width] + pair[:, width:]


def apply_kernel(sub, d_ref, row_ref, col_ref, a_ref, lower_ref, upper_ref, xs, xl, ys):
    step = pl.program_id(0)
    depth, size = a_ref.shape[1:]
    half = size // 2

    @pl.when(step == 0)
    def _():
        put_split(xs, pl.ds(0, half), -d_ref[sub])
        put_split(xs, pl.ds(half, half), d_ref[sub + 1])
        spots = row_ref[...]

        @pl.loop(0, size // depth)
        def _(b):
            start = pl.multiple_of(b * depth, depth)
            want = lax.broadcasted_iota(jnp.int32, (depth, size), 0) + start
            table = jnp.where(want == spots, 1.0, 0.0).astype(bf16)
            xl[pl.ds(start, depth), :] = jnp.dot(
                table, xs[...], preferred_element_type=f32
            ).astype(bf16)

    block = a_ref[0]
    high = block.astype(bf16)
    low = (block - high.astype(f32)).astype(bf16)
    vector = xl[...]
    pair = jnp.dot(high, vector, preferred_element_type=f32) + jnp.dot(
        low, vector, preferred_element_type=f32
    )
    put_split(ys, pl.ds(pl.multiple_of(step * depth, depth), depth), joined_halves(pair))

    @pl.when(step == size // depth - 1)
    def _():
        for side, out_ref in enumerate((lower_ref, upper_ref)):

            @pl.loop(0, half // depth)
            def _(b):
                start = pl.multiple_of(b * depth, depth)
                spots = col_ref[pl.ds(side * half + start, depth), :]
                lane = lax.broadcasted_iota(jnp.int32, (depth, size), 1)
                table = jnp.where(lane == spots, 1.0, 0.0).astype(bf16)
                out_ref[pl.ds(start, depth), :] = joined_halves(
                    jnp.dot(table, ys[...], preferred_element_type=f32)
                )


def apply_operator(direction, row_perm, col_perm, dual_ops, sub):
    size = dual_ops.shape[1]
    half, width = direction.shape[1:]
    depth = next(d for d in (256, 128, 64, 32, 16) if half % d == 0)
    return pl.pallas_call(
        functools.partial(apply_kernel, sub),
        grid=(size // depth,),
        out_shape=[jax.ShapeDtypeStruct((half, width), f32)] * 2,
        in_specs=[
            pl.BlockSpec(direction.shape, lambda i: (0, 0, 0)),
            pl.BlockSpec((None, 1, size), lambda i: (sub, 0, 0)),
            pl.BlockSpec((None, size, 1), lambda i: (sub, 0, 0)),
            pl.BlockSpec((1, depth, size), lambda i: (sub, i, 0)),
        ],
        out_specs=[pl.BlockSpec((half, width), lambda i: (0, 0))] * 2,
        scratch_shapes=[pltpu.VMEM((size, 2 * width), bf16)] * 3,
        cost_estimate=pl.CostEstimate(
            flops=16 * size * size * width, bytes_accessed=4 * size * size, transcendentals=0
        ),
        compiler_params=pltpu.CompilerParams(vmem_limit_bytes=40 * 2**20),
    )(direction, row_perm, col_perm, dual_ops)


def split(value, axis):
    high = lax.reduce_precision(value, 8, 7)
    return jnp.concatenate([high.astype(bf16), (value - high).astype(bf16)], axis=axis)


def unsplit(pair):
    width = pair.shape[-1] // 2
    return pair[..., :width] + pair[..., width:]


def shards(dual_ops, modes, coarse_rows, coarse_cols, row_perm, iface_size, rhs):
    sub_count, half_width, case_count = rhs.shape
    size = 2 * half_width
    mode_count = modes.shape[1]
    dom_count = lax.axis_size("dom") * sub_count
    row_view = row_perm[:, None, :]
    col_view = row_perm[:, :, None]
    block_count = coarse_cols.shape[1]
    int_pack = jnp.concatenate([coarse_cols, iface_size[:, None]], axis=1)
    live_own = (
        lax.broadcasted_iota(jnp.int32, (sub_count, half_width), 1) < iface_size[:, None]
    ).astype(f32)[:, :, None]
    start_vector = rhs * live_own
    prior_rim = from_behind(start_vector[-1], "dom", 1)
    prior_ints = from_behind(int_pack[-1], "dom", 1)
    next_ints = from_behind(int_pack[0], "dom", -1)
    permutation = (
        row_perm[:, :, None] == lax.broadcasted_iota(jnp.int32, (1, 1, size), 2)
    ).astype(bf16)
    slot_modes = jnp.einsum("sjn,skn->sjk", modes, permutation, preferred_element_type=f32).astype(
        bf16
    )
    prior_modes = from_behind(slot_modes[-1], "dom", 1)
    next_modes = from_behind(slot_modes[0], "dom", -1)
    prior_blocks = from_behind(coarse_rows[-1], "dom", 1)
    next_blocks = from_behind(coarse_rows[0], "dom", -1)
    ext_ints = jnp.concatenate([prior_ints[None], int_pack, next_ints[None]], axis=0)
    ext_cols = ext_ints[:, :block_count]
    ext_size = ext_ints[:-1, block_count]
    ext_modes = jnp.concatenate([prior_modes[None], slot_modes, next_modes[None]], axis=0)
    ext_blocks = jnp.concatenate([prior_blocks[None], coarse_rows, next_blocks[None]], axis=0)
    live = (
        lax.broadcasted_iota(jnp.int32, (sub_count + 1, half_width), 1) < ext_size[:, None]
    ).astype(f32)[:, :, None]
    column_table = (
        ext_cols[:, :, None] == lax.broadcasted_iota(jnp.int32, (1, 1, dom_count), 2)
    ).astype(f32)
    coarse = jnp.einsum("sqij,sqd->sidj", ext_blocks, column_table, precision=highest).reshape(
        (sub_count + 2) * mode_count, dom_count * mode_count
    )
    fit_modes = jnp.concatenate([-slot_modes[:, :, :half_width], slot_modes[:, :, half_width:]], 2)
    join_modes = jnp.concatenate(
        [ext_modes[:-1, :, half_width:], -ext_modes[1:, :, :half_width]], axis=1
    )

    def correction_of(vector):
        pairs = split(vector, 2)
        locals_ = jnp.concatenate([pairs[:-1], pairs[1:]], axis=1)
        coefficients = unsplit(
            jnp.einsum("sjn,snc->sjc", fit_modes, locals_, preferred_element_type=f32)
        ).astype(bf16)
        everyone = push_gather(coefficients, ("dom",), 1).reshape(
            dom_count * mode_count, case_count
        )
        amounts = jnp.dot(coarse, everyone.astype(f32), precision=highest)
        amounts = split(amounts, 1).reshape(sub_count + 2, mode_count, 2 * case_count)
        amounts = jnp.concatenate([amounts[:-1], amounts[1:]], axis=1)
        return live * unsplit(
            jnp.einsum("sjn,sjc->snc", join_modes, amounts, preferred_element_type=f32)
        )

    centre = 0.5 * (high_bound + low_bound)
    radius = 0.5 * (high_bound - low_bound)
    spread_ratio = centre / radius
    ratio_now = 1.0 / spread_ratio
    residual = jnp.concatenate([prior_rim[None], start_vector], axis=0)
    residual = residual - correction_of(residual)
    direction = residual / centre
    solution = jnp.zeros_like(rhs)
    sums = []
    for turn_index in range(STEPS):
        solution = solution + direction[1:]
        lowers, uppers = [None] * sub_count, [None] * sub_count
        order = [sub_count - 1] + list(range(sub_count - 1))
        for sub in order:
            lowers[sub], uppers[sub] = apply_operator(direction, row_view, col_view, dual_ops, sub)
        uppers = [from_behind(uppers[-1], "dom", 1)] + uppers
        lowers = lowers + [from_behind(lowers[0], "dom", -1)]
        mapped = jnp.stack([u - l for u, l in zip(uppers, lowers)]) * live
        residual = residual - (mapped - correction_of(mapped))
        sums.append(jnp.sum(residual[1:] * residual[1:], axis=(0, 1)))
        if turn_index + 1 < STEPS:
            ratio_next = 1.0 / (2.0 * spread_ratio - ratio_now)
            direction = ratio_next * ratio_now * direction + 2.0 * ratio_next / radius * residual
            ratio_now = ratio_next
    rows = -(-STEPS // 8) * 8
    pack = jnp.zeros((rows, case_count), f32).at[:STEPS].set(jnp.stack(sums))
    cases = lax.axis_size("case")
    everyone = push_gather(pack, ("dom", "case"), 2).reshape(-1, cases, rows, case_count)
    norms = jnp.sqrt(jnp.sum(everyone, axis=0)[:, :STEPS] + epsilon)
    history = lax.dynamic_index_in_dim(norms, lax.axis_index("case"), 0, keepdims=False)
    peak_norm = jnp.max(norms, axis=(0, 2))
    return (solution, residual[1:], history, peak_norm)


def solution(mesh):
    in_specs = (
        P("dom", None, None),
        P("dom", None, None),
        P("dom", None, None, None),
        P("dom", None),
        P("dom", None),
        P("dom"),
        P("dom", None, "case"),
    )
    out_specs = (P("dom", None, "case"), P("dom", None, "case"), P(None, "case"), P())
    return jax.shard_map(shards, mesh=mesh, in_specs=in_specs, out_specs=out_specs, check_vma=False)
```

time: 606 us -> 277 us (0.46)
  blocking collectives: 178 us -> 0 us
  local copies, waits for them, and re-layouts: 181 us -> 9.98 us
  Pallas kernels: 0 us -> 149 us
  matrix products: 156 us -> 14.2 us
  waiting for transfers between devices: 44.9 us -> 57.8 us
    gather x6 -> x0, local copies, waits for them, and re-layouts: 172 us -> none  [the longest x3 155 us: shards(): matrix[ordering].T[ordering]]
    all_gather x5 -> x0, blocking collectives: 153 us -> none  [gather_coefficients(): return lax.all_gather(coefficients, 'dom', axis=0, tiled=True)]
    pallas_call x0 -> x14, Pallas kernels: none -> 149 us  [the longest x8 99.4 us: apply_operator(): pl.pallas_call(functools.partial(apply_kernel, sub), grid=(size // depth,...]
    dot_general x24 -> x17, matrix products: 156 us -> 14.2 us  [the longest x5 5.08 us: correction_of(): amounts = jnp.dot(coarse, everyone.astype(f32), precision=highest)]
    psum x1 -> x0, blocking collectives: 19.1 us -> none  [shards(): norm_list.append(jnp.sqrt(lax.psum(partial_value, 'dom') + epsilon))]
    ppermute x17 -> x15, waiting for transfers between devices: 44.9 us -> 57.8 us  [from_behind(): return lax.ppermute(block, axis, route)]
    pmax x1 -> x0, blocking collectives: 6.16 us -> none  [shards(): peak_norm = lax.pmax(jnp.max(history, axis=1), 'case')]
    ppermute x17 -> x15, starting transfers between devices: 24.5 us -> 22.3 us  [from_behind(): return lax.ppermute(block, axis, route)]
  transfers between devices with their start and end apart: 17 -> 15, of which waited for: 9 -> 6; matrix products, arithmetic and copies ran while one was open for 35% -> 6% of each run, Pallas kernels for 0% -> 7%
where the time goes in v1:
time: 277 us; the launch traced here: 275 us
  Pallas kernels  149 us (54%)
  waiting for transfers between devices  57.8 us (21%)
  starting transfers between devices  22.3 us (8%)
  other arithmetic  20.4 us (7%)
  matrix products  14.2 us (5%)
  local copies, waits for them, and re-layouts  9.98 us (4%)
    pallas_call x8, Pallas kernels, apply_operator(): pl.pallas_call(functools.partial(apply_kernel, sub), grid=(size // depth,...  99.4 us
    ppermute x15, waiting for transfers between devices, from_behind(): return lax.ppermute(block, axis, route)  57.8 us
    pallas_call x6, Pallas kernels, push_gather(): pl.pallas_call(functools.partial(gather_kernel, axes, sizes), out_shape=j...  49.9 us
    ppermute x15, starting transfers between devices, from_behind(): return lax.ppermute(block, axis, route)  22.3 us
  transfers between devices with their start and end apart: 15, of which 6 were waited for; matrix products, arithmetic and copies ran while one was open for 6% of the time, Pallas kernels for 7%

profile of v1, /device:TPU:0, one launch (start us, length us, event | category | flops | bytes accessed | tf_op | source)
XLA Modules:
  0.0 275.3 jit_solution(4951344850798698148)
XLA Ops:
  2.2 3.0 %collective-permute-start.1 = (s32[9]{0:T(128)S(1)}, s32[9]{0:T(128)S(1)}, u32[]{:S(2)}, u32[]{:S(2)}) collective-permute-start(s32[9]{0:T(128)S(1)} %get-tuple-element.99), channel_id=1, source_target_pairs={{28,0},{0,4},{4,8},{8,12},{12,16},{16,20},{20,24},{24,28},{29,1},{... | collective-permute-start | bytes 116 | tf_op jit(solution)/shard_map/ppermute | solution.py:23
  5.2 3.1 %collective-permute-start.4 = (s32[9]{0:T(128)S(1)}, s32[9]{0:T(128)S(1)}, u32[]{:S(2)}, u32[]{:S(2)}) collective-permute-start(s32[9]{0:T(128)S(1)} %get-tuple-element.100), channel_id=1, source_target_pairs={{4,0},{8,4},{12,8},{16,12},{20,16},{24,20},{28,24},{0,28},{5,1},{9... | collective-permute-start | bytes 116 | tf_op jit(solution)/shard_map/ppermute | solution.py:23
  8.3 4.5 %fusion.3 = bf16[2,16,1536]{2,1,0:T(8,128)(2,1)S(1)} fusion(bf16[2,16,1536]{2,1,0:T(8,128)(2,1)S(1)} %copy-done, s32[2,1536]{1,0:T(2,128)} %param.13), kind=kOutput, calls=%fused_computation.4 | convolution fusion | flops 155762688 | bytes 208896 | tf_op jit(solution)/shard_map/sjn,skn->sjk/dot_general | solution.py:194
  13.5 1.9 collective-permute-start.3
  17.9 4.8 %collective-permute-start.6 = (f32[8,16,16]{2,0,1:T(8,128)S(1)}, f32[8,16,16]{2,0,1:T(8,128)S(1)}, u32[]{:S(2)}, u32[]{:S(2)}) collective-permute-start(f32[8,16,16]{2,0,1:T(8,128)S(1)} %get-tuple-element.72), channel_id=1, source_target_pairs={{4,0},{8,4},{12,8},{16,12},{20,16},{24,20},{28,24},{0,28},{5,1},{9... | collective-permute-start | bytes 24584 | tf_op jit(solution)/shard_map/ppermute | solution.py:23
  25.4 10.1 %collective-permute-done = f32[768,128]{1,0:T(8,128)} collective-permute-done((f32[768,128]{1,0:T(8,128)}, f32[768,128]{1,0:T(8,128)}, u32[]{:S(2)}, u32[]{:S(2)}) %collective-permute-start) | collective-permute-done | bytes 393248 | tf_op jit(solution)/shard_map/ppermute | solution.py:23
  38.4 7.8 %shard_map.102 = bf16[8,2,16,128]{3,2,1,0:T(8,128)(2,1)} custom-call(bf16[2,16,128]{2,1,0:T(8,128)(2,1)} %fusion.85.x_ref), custom_call_target="tpu_custom_call" | custom-call | tf_op jit(solution)/shard_map/pallas_call | solution.py:72
  47.8 2.4 broadcast_multiply_fusion
  50.2 12.6 %shard_map.104 = (f32[768,128]{1,0:T(8,128)S(1)}, f32[768,128]{1,0:T(8,128)S(1)}) custom-call(f32[3,768,128]{2,1,0:T(8,128)S(1)} %get-tuple-element.58.d_ref, s32[2,1,1536]{2,1,0:T(1,128)S(1)} %broadcast_in_dim.44.row_ref, s32[2,1536,1]{2,1,0:T(8,128)S(1)} %copy.19.col_ref, f32[2,1536,1536]{2,1,0:T(8,128)} %a_ref.15), custom_call_target="tpu_custom_call" | custom-call | flops 4831838208 | bytes 9437184 | tf_op jit(solution)/shard_map/pallas_call | solution.py:146
  62.8 1.2 collective-permute-start.8
  64.1 12.2 %shard_map.103 = (f32[768,128]{1,0:T(8,128)S(1)}, f32[768,128]{1,0:T(8,128)S(1)}) custom-call(f32[3,768,128]{2,1,0:T(8,128)S(1)} %get-tuple-element.58.d_ref, s32[2,1,1536]{2,1,0:T(1,128)S(1)} %broadcast_in_dim.44.row_ref, s32[2,1536,1]{2,1,0:T(8,128)S(1)} %copy.19.col_ref, f32[2,1536,1536]{2,1,0:T(8,128)} %a_ref.15), custom_call_target="tpu_custom_call" | custom-call | flops 4831838208 | bytes 9437184 | tf_op jit(solution)/shard_map/pallas_call | solution.py:146
  77.5 9.5 %collective-permute-done.7 = f32[768,128]{1,0:T(8,128)S(1)} collective-permute-done((f32[768,128]{1,0:T(8,128)S(1)}, f32[768,128]{1,0:T(8,128)S(1)}, u32[]{:S(2)}, u32[]{:S(2)}) %collective-permute-start.7) | collective-permute-done | bytes 393248 | tf_op jit(solution)/shard_map/ppermute | solution.py:23
  88.4 7.8 %shard_map.105 = bf16[8,2,16,128]{3,2,1,0:T(8,128)(2,1)} custom-call(bf16[2,16,128]{2,1,0:T(8,128)(2,1)} %fusion.84.x_ref), custom_call_target="tpu_custom_call" | custom-call | tf_op jit(solution)/shard_map/pallas_call | solution.py:72
  99.1 13.0 %shard_map.107 = (f32[768,128]{1,0:T(8,128)S(1)}, f32[768,128]{1,0:T(8,128)S(1)}) custom-call(f32[3,768,128]{2,1,0:T(8,128)S(1)} %get-tuple-element.56.d_ref, s32[2,1,1536]{2,1,0:T(1,128)S(1)} %broadcast_in_dim.44.row_ref, s32[2,1536,1]{2,1,0:T(8,128)S(1)} %copy.19.col_ref, f32[2,1536,1536]{2,1,0:T(8,128)} %a_ref.15), custom_call_target="tpu_custom_call" | custom-call | flops 4831838208 | bytes 9437184 | tf_op jit(solution)/shard_map/pallas_call | solution.py:146
  112.1 12.2 %shard_map.106 = (f32[768,128]{1,0:T(8,128)S(1)}, f32[768,128]{1,0:T(8,128)S(1)}) custom-call(f32[3,768,128]{2,1,0:T(8,128)S(1)} %get-tuple-element.56.d_ref, s32[2,1,1536]{2,1,0:T(1,128)S(1)} %broadcast_in_dim.44.row_ref, s32[2,1536,1]{2,1,0:T(8,128)S(1)} %copy.19.col_ref, f32[2,1536,1536]{2,1,0:T(8,128)} %a_ref.15), custom_call_target="tpu_custom_call" | custom-call | flops 4831838208 | bytes 9437184 | tf_op jit(solution)/shard_map/pallas_call | solution.py:146
  124.3 1.2 collective-permute-start.10
  127.2 10.5 %collective-permute-done.10 = f32[768,128]{1,0:T(8,128)S(1)} collective-permute-done((f32[768,128]{1,0:T(8,128)S(1)}, f32[768,128]{1,0:T(8,128)S(1)}, u32[]{:S(2)}, u32[]{:S(2)}) %collective-permute-start.10) | collective-permute-done | bytes 393248 | tf_op jit(solution)/shard_map/ppermute | solution.py:23
  139.6 7.8 %shard_map.108 = bf16[8,2,16,128]{3,2,1,0:T(8,128)(2,1)} custom-call(bf16[2,16,128]{2,1,0:T(8,128)(2,1)} %fusion.83.x_ref), custom_call_target="tpu_custom_call" | custom-call | tf_op jit(solution)/shard_map/pallas_call | solution.py:72
  150.2 1.4 multiply_add_fusion.1
  151.6 12.6 %shard_map.110 = (f32[768,128]{1,0:T(8,128)S(1)}, f32[768,128]{1,0:T(8,128)S(1)}) custom-call(f32[3,768,128]{2,1,0:T(8,128)S(1)} %get-tuple-element.54.d_ref, s32[2,1,1536]{2,1,0:T(1,128)S(1)} %broadcast_in_dim.44.row_ref, s32[2,1536,1]{2,1,0:T(8,128)S(1)} %copy.19.col_ref, f32[2,1536,1536]{2,1,0:T(8,128)} %a_ref.15), custom_call_target="tpu_custom_call" | custom-call | flops 4831838208 | bytes 9437184 | tf_op jit(solution)/shard_map/pallas_call | solution.py:146
  164.2 12.2 %shard_map.109 = (f32[768,128]{1,0:T(8,128)S(1)}, f32[768,128]{1,0:T(8,128)S(1)}) custom-call(f32[3,768,128]{2,1,0:T(8,128)S(1)} %get-tuple-element.54.d_ref, s32[2,1,1536]{2,1,0:T(1,128)S(1)} %broadcast_in_dim.44.row_ref, s32[2,1536,1]{2,1,0:T(8,128)S(1)} %copy.19.col_ref, f32[2,1536,1536]{2,1,0:T(8,128)} %a_ref.15), custom_call_target="tpu_custom_call" | custom-call | flops 4831838208 | bytes 9437184 | tf_op jit(solution)/shard_map/pallas_call | solution.py:146
  176.4 2.5 collective-permute-start.12
  179.7 12.7 %collective-permute-done.12 = f32[768,128]{1,0:T(8,128)S(1)} collective-permute-done((f32[768,128]{1,0:T(8,128)S(1)}, f32[768,128]{1,0:T(8,128)S(1)}, u32[]{:S(2)}, u32[]{:S(2)}) %collective-permute-start.12) | collective-permute-done | bytes 393248 | tf_op jit(solution)/shard_map/ppermute | solution.py:23
  194.3 8.0 %shard_map.111 = bf16[8,2,16,128]{3,2,1,0:T(8,128)(2,1)} custom-call(bf16[2,16,128]{2,1,0:T(8,128)(2,1)} %fusion.82.x_ref), custom_call_target="tpu_custom_call" | custom-call | tf_op jit(solution)/shard_map/pallas_call | solution.py:72
  204.9 1.4 multiply_add_fusion
  206.3 12.2 %shard_map.113 = (f32[768,128]{1,0:T(8,128)S(1)}, f32[768,128]{1,0:T(8,128)S(1)}) custom-call(f32[3,768,128]{2,1,0:T(8,128)S(1)} %get-tuple-element.52.d_ref, s32[2,1,1536]{2,1,0:T(1,128)S(1)} %broadcast_in_dim.44.row_ref, s32[2,1536,1]{2,1,0:T(8,128)S(1)} %copy.19.col_ref, f32[2,1536,1536]{2,1,0:T(8,128)} %a_ref.15), custom_call_target="tpu_custom_call" | custom-call | flops 4831838208 | bytes 9437184 | tf_op jit(solution)/shard_map/pallas_call | solution.py:146
  218.5 12.4 %shard_map.112 = (f32[768,128]{1,0:T(8,128)S(1)}, f32[768,128]{1,0:T(8,128)S(1)}) custom-call(f32[3,768,128]{2,1,0:T(8,128)S(1)} %get-tuple-element.52.d_ref, s32[2,1,1536]{2,1,0:T(1,128)S(1)} %broadcast_in_dim.44.row_ref, s32[2,1536,1]{2,1,0:T(8,128)S(1)} %copy.19.col_ref, f32[2,1536,1536]{2,1,0:T(8,128)} %a_ref.15), custom_call_target="tpu_custom_call" | custom-call | flops 4831838208 | bytes 9437184 | tf_op jit(solution)/shard_map/pallas_call | solution.py:146
  230.9 2.4 collective-permute-start.14
  234.4 14.1 %collective-permute-done.14 = f32[768,128]{1,0:T(8,128)S(1)} collective-permute-done((f32[768,128]{1,0:T(8,128)S(1)}, f32[768,128]{1,0:T(8,128)S(1)}, u32[]{:S(2)}, u32[]{:S(2)}) %collective-permute-start.14) | collective-permute-done | bytes 393248 | tf_op jit(solution)/shard_map/ppermute | solution.py:23
  250.1 8.8 %shard_map.114 = bf16[8,2,16,128]{3,2,1,0:T(8,128)(2,1)} custom-call(bf16[2,16,128]{2,1,0:T(8,128)(2,1)} %fusion.81.x_ref), custom_call_target="tpu_custom_call" | custom-call | tf_op jit(solution)/shard_map/pallas_call | solution.py:72
  261.7 1.2 multiply_reduce_fusion
  263.5 9.6 %shard_map.115 = f32[32,8,128]{2,1,0:T(8,128)} custom-call(f32[8,128]{1,0:T(8,128)} %select_maximum_fusion.x_ref), custom_call_target="tpu_custom_call" | custom-call | tf_op jit(solution)/shard_map/pallas_call | solution.py:72
  (152 shorter events, 36.6 us)
Async XLA Ops:
  0.6 7.7 %copy-start = (bf16[2,16,1536]{2,1,0:T(8,128)(2,1)S(1)}, bf16[2,16,1536]{2,1,0:T(8,128)(2,1)}, u32[]{:S(2)}) copy-start(bf16[2,16,1536]{2,1,0:T(8,128)(2,1)} %param.10) | copy-start | bytes 294916
  2.2 15.8 %collective-permute-start.1 = (s32[9]{0:T(128)S(1)}, s32[9]{0:T(128)S(1)}, u32[]{:S(2)}, u32[]{:S(2)}) collective-permute-start(s32[9]{0:T(128)S(1)} %get-tuple-element.99), channel_id=1, source_target_pairs={{28,0},{0,4},{4,8},{8,12},{12,16},{16,20},{20,24},{24,28},{29,1},{... | collective-permute-start | bytes 116 | tf_op jit(solution)/shard_map/ppermute | solution.py:23
  5.2 10.3 %copy-start.21 = (f32[2,8,16,16]{3,2,1,0:T(8,128)S(1)}, f32[2,8,16,16]{3,2,1,0:T(8,128)}, u32[]{:S(2)}) copy-start(f32[2,8,16,16]{3,2,1,0:T(8,128)} %param.11) | copy-start | bytes 49156
  5.2 10.5 %copy-start.28 = (s32[2]{0:T(128)S(1)}, s32[2]{0:T(128)}, u32[]{:S(2)}) copy-start(s32[2]{0:T(128)} %param.14) | copy-start | bytes 28
  5.2 10.5 %copy-start.22 = (s32[2,1536]{1,0:T(2,128)S(1)}, s32[2,1536]{1,0:T(2,128)}, u32[]{:S(2)}) copy-start(s32[2,1536]{1,0:T(2,128)} %param.13) | copy-start | bytes 36868
  5.2 17.9 %collective-permute-start.4 = (s32[9]{0:T(128)S(1)}, s32[9]{0:T(128)S(1)}, u32[]{:S(2)}, u32[]{:S(2)}) collective-permute-start(s32[9]{0:T(128)S(1)} %get-tuple-element.100), channel_id=1, source_target_pairs={{4,0},{8,4},{12,8},{16,12},{20,16},{24,20},{28,24},{0,28},{5,1},{9... | collective-permute-start | bytes 116 | tf_op jit(solution)/shard_map/ppermute | solution.py:23
  12.8 3.6 %copy-start.20 = (f32[2,768,128]{2,1,0:T(8,128)S(1)}, f32[2,768,128]{2,1,0:T(8,128)}, u32[]{:S(2)}) copy-start(f32[2,768,128]{2,1,0:T(8,128)} %param.15) | copy-start | bytes 2359300
  13.5 11.9 %collective-permute-start.3 = (bf16[16,1536]{1,0:T(8,128)(2,1)}, bf16[16,1536]{1,0:T(8,128)(2,1)S(1)}, u32[]{:S(2)}, u32[]{:S(2)}) collective-permute-start(bf16[16,1536]{1,0:T(8,128)(2,1)} %get-tuple-element.73), channel_id=1, source_target_pairs={{4,0},{8,4},{12,8},{16,12},{20,16},{24,20},{28,24},{0,28},{5,1},{9... | collective-permute-start | bytes 147464 | tf_op jit(solution)/shard_map/ppermute | solution.py:23
  15.4 31.9 %collective-permute-start.2 = (bf16[16,1536]{1,0:T(8,128)(2,1)}, bf16[16,1536]{1,0:T(8,128)(2,1)S(1)}, u32[]{:S(2)}, u32[]{:S(2)}) collective-permute-start(bf16[16,1536]{1,0:T(8,128)(2,1)} %get-tuple-element.74), channel_id=1, source_target_pairs={{28,0},{0,4},{4,8},{8,12},{12,16},{16,20},{20,24},{24,28},{29,1},{... | collective-permute-start | bytes 147464 | tf_op jit(solution)/shard_map/ppermute | solution.py:23
  15.6 8.2 %collective-permute-start.5 = (f32[8,16,16]{2,0,1:T(8,128)S(1)}, f32[8,16,16]{2,0,1:T(8,128)S(1)}, u32[]{:S(2)}, u32[]{:S(2)}) collective-permute-start(f32[8,16,16]{2,0,1:T(8,128)S(1)} %get-tuple-element.71), channel_id=1, source_target_pairs={{28,0},{0,4},{4,8},{8,12},{12,16},{16,20},{20,24},{24,28},{29,1},{... | collective-permute-start | bytes 24584 | tf_op jit(solution)/shard_map/ppermute | solution.py:23
  16.6 6.1 %copy-start.25 = (s32[2,8]{1,0:T(2,128)S(1)}, s32[2,8]{1,0:T(2,128)}, u32[]{:S(2)}) copy-start(s32[2,8]{1,0:T(2,128)} %param.12) | copy-start | bytes 196
  17.9 6.7 %collective-permute-start.6 = (f32[8,16,16]{2,0,1:T(8,128)S(1)}, f32[8,16,16]{2,0,1:T(8,128)S(1)}, u32[]{:S(2)}, u32[]{:S(2)}) collective-permute-start(f32[8,16,16]{2,0,1:T(8,128)S(1)} %get-tuple-element.72), channel_id=1, source_target_pairs={{4,0},{8,4},{12,8},{16,12},{20,16},{24,20},{28,24},{0,28},{5,1},{9... | collective-permute-start | bytes 24584 | tf_op jit(solution)/shard_map/ppermute | solution.py:23
  23.0 12.5 %collective-permute-start = (f32[768,128]{1,0:T(8,128)}, f32[768,128]{1,0:T(8,128)}, u32[]{:S(2)}, u32[]{:S(2)}) collective-permute-start(f32[768,128]{1,0:T(8,128)} %slice_bitcast_fusion), channel_id=1, source_target_pairs={{28,0},{0,4},{4,8},{8,12},{12,16},{16,20},{20,24},{24,28},{29,1},{... | collective-permute-start | bytes 1179656 | tf_op jit(solution)/shard_map/ppermute | solution.py:23
  50.2 13.8 %copy-start.5 = (f32[3,768,128]{2,1,0:T(8,128)}, f32[3,768,128]{2,1,0:T(8,128)S(1)}, u32[]{:S(2)}) copy-start(f32[3,768,128]{2,1,0:T(8,128)S(1)} %get-tuple-element.58.d_ref) | copy-start | bytes 3538948
  62.8 14.6 %collective-permute-start.8 = (f32[768,128]{1,0:T(8,128)S(1)}, f32[768,128]{1,0:T(8,128)S(1)}, u32[]{:S(2)}, u32[]{:S(2)}) collective-permute-start(f32[768,128]{1,0:T(8,128)S(1)} %get-tuple-element.33), channel_id=1, source_target_pairs={{4,0},{8,4},{12,8},{16,12},{20,16},{24,20},{28,24},{0,28},{5,1},{9... | collective-permute-start | bytes 1179656 | tf_op jit(solution)/shard_map/ppermute | solution.py:23
  76.3 10.7 %collective-permute-start.7 = (f32[768,128]{1,0:T(8,128)S(1)}, f32[768,128]{1,0:T(8,128)S(1)}, u32[]{:S(2)}, u32[]{:S(2)}) collective-permute-start(f32[768,128]{1,0:T(8,128)S(1)} %get-tuple-element.32), channel_id=1, source_target_pairs={{28,0},{0,4},{4,8},{8,12},{12,16},{16,20},{20,24},{24,28},{29,1},{... | collective-permute-start | bytes 1179656 | tf_op jit(solution)/shard_map/ppermute | solution.py:23
  99.0 13.1 %copy-start.2 = (f32[3,768,128]{2,1,0:T(8,128)}, f32[3,768,128]{2,1,0:T(8,128)S(1)}, u32[]{:S(2)}) copy-start(f32[3,768,128]{2,1,0:T(8,128)S(1)} %get-tuple-element.56.d_ref) | copy-start | bytes 3538948
  99.0 27.4 %copy-start.9 = (f32[3,768,128]{2,1,0:T(8,128)}, f32[3,768,128]{2,1,0:T(8,128)S(1)}, u32[]{:S(2)}) copy-start(f32[3,768,128]{2,1,0:T(8,128)S(1)} %get-tuple-element.57) | copy-start | bytes 3538948
  124.3 13.4 %collective-permute-start.10 = (f32[768,128]{1,0:T(8,128)S(1)}, f32[768,128]{1,0:T(8,128)S(1)}, u32[]{:S(2)}, u32[]{:S(2)}) collective-permute-start(f32[768,128]{1,0:T(8,128)S(1)} %get-tuple-element.37), channel_id=1, source_target_pairs={{4,0},{8,4},{12,8},{16,12},{20,16},{24,20},{28,24},{0,28},{5,1},{9... | collective-permute-start | bytes 1179656 | tf_op jit(solution)/shard_map/ppermute | solution.py:23
  125.5 12.2 %collective-permute-start.9 = (f32[768,128]{1,0:T(8,128)S(1)}, f32[768,128]{1,0:T(8,128)S(1)}, u32[]{:S(2)}, u32[]{:S(2)}) collective-permute-start(f32[768,128]{1,0:T(8,128)S(1)} %get-tuple-element.36), channel_id=1, source_target_pairs={{28,0},{0,4},{4,8},{8,12},{12,16},{16,20},{20,24},{24,28},{29,1},{... | collective-permute-start | bytes 1179656 | tf_op jit(solution)/shard_map/ppermute | solution.py:23
  147.5 1.6 copy-start.13
  148.6 1.6 copy-start.10
  151.6 27.4 %copy-start.7 = (f32[3,768,128]{2,1,0:T(8,128)}, f32[3,768,128]{2,1,0:T(8,128)S(1)}, u32[]{:S(2)}) copy-start(f32[3,768,128]{2,1,0:T(8,128)S(1)} %get-tuple-element.55) | copy-start | bytes 3538948
  176.4 16.0 %collective-permute-start.12 = (f32[768,128]{1,0:T(8,128)S(1)}, f32[768,128]{1,0:T(8,128)S(1)}, u32[]{:S(2)}, u32[]{:S(2)}) collective-permute-start(f32[768,128]{1,0:T(8,128)S(1)} %get-tuple-element.41), channel_id=1, source_target_pairs={{4,0},{8,4},{12,8},{16,12},{20,16},{24,20},{28,24},{0,28},{5,1},{9... | collective-permute-start | bytes 1179656 | tf_op jit(solution)/shard_map/ppermute | solution.py:23
  178.9 13.5 %collective-permute-start.11 = (f32[768,128]{1,0:T(8,128)S(1)}, f32[768,128]{1,0:T(8,128)S(1)}, u32[]{:S(2)}, u32[]{:S(2)}) collective-permute-start(f32[768,128]{1,0:T(8,128)S(1)} %get-tuple-element.40), channel_id=1, source_target_pairs={{28,0},{0,4},{4,8},{8,12},{12,16},{16,20},{20,24},{24,28},{29,1},{... | collective-permute-start | bytes 1179656 | tf_op jit(solution)/shard_map/ppermute | solution.py:23
  203.4 1.3 copy-start.15
  203.4 1.4 copy-start.18
  218.5 14.8 %copy-start.4 = (f32[3,768,128]{2,1,0:T(8,128)S(1)}, f32[3,768,128]{2,1,0:T(8,128)}, u32[]{:S(2)}) copy-start(f32[3,768,128]{2,1,0:T(8,128)} %copy-done.2) | copy-start | bytes 3538948
  218.5 14.8 %copy-start.6 = (f32[3,768,128]{2,1,0:T(8,128)S(1)}, f32[3,768,128]{2,1,0:T(8,128)}, u32[]{:S(2)}) copy-start(f32[3,768,128]{2,1,0:T(8,128)} %copy-done.5) | copy-start | bytes 3538948
  230.9 17.5 %collective-permute-start.14 = (f32[768,128]{1,0:T(8,128)S(1)}, f32[768,128]{1,0:T(8,128)S(1)}, u32[]{:S(2)}, u32[]{:S(2)}) collective-permute-start(f32[768,128]{1,0:T(8,128)S(1)} %get-tuple-element.45), channel_id=1, source_target_pairs={{4,0},{8,4},{12,8},{16,12},{20,16},{24,20},{28,24},{0,28},{5,1},{9... | collective-permute-start | bytes 1179656 | tf_op jit(solution)/shard_map/ppermute | solution.py:23
  234.3 14.2 %collective-permute-start.13 = (f32[768,128]{1,0:T(8,128)S(1)}, f32[768,128]{1,0:T(8,128)S(1)}, u32[]{:S(2)}, u32[]{:S(2)}) collective-permute-start(f32[768,128]{1,0:T(8,128)S(1)} %get-tuple-element.44), channel_id=1, source_target_pairs={{28,0},{0,4},{4,8},{8,12},{12,16},{16,20},{20,24},{24,28},{29,1},{... | collective-permute-start | bytes 1179656 | tf_op jit(solution)/shard_map/ppermute | solution.py:23
  260.6 14.7 %copy-start.1 = (bf16[2,16,1536]{2,1,0:T(8,128)(2,1)S(1)}, bf16[2,16,1536]{2,1,0:T(8,128)(2,1)}, u32[]{:S(2)}) copy-start(bf16[2,16,1536]{2,1,0:T(8,128)(2,1)} %param.10) | copy-start | bytes 294916
  (12 other events, 12.7 us)

commit v2 on v1

--- a/solution.py
+++ b/solution.py
@@ -95,71 +95,106 @@
     return pair[:, :width] + pair[:, width:]
 
 
-def apply_kernel(sub, d_ref, row_ref, col_ref, a_ref, lower_ref, upper_ref, xs, xl, ys):
+def setup_kernel(row_ref, col_ref, a_ref, out_ref, diagonal_ref, rest, table, diagonal):
+    depth, size = out_ref.shape
+
+    @pl.when(pl.program_id(1) == 0)
+    def _():
+        spots = row_ref[...]
+        diagonal[...] = jnp.zeros_like(diagonal)
+
+        @pl.loop(0, size // depth)
+        def _(b):
+            start = pl.multiple_of(b * depth, depth)
+            row = lax.broadcasted_iota(jnp.int32, (depth, size), 0) + start
+            same = row == lax.broadcasted_iota(jnp.int32, (depth, size), 1)
+            block = a_ref[pl.ds(start, depth), :]
+            diagonal[...] += jnp.sum(jnp.where(same, block, 0.0), axis=0, keepdims=True)
+            rest[pl.ds(start, depth), :] = jnp.where(same, 0.0, block).astype(bf16)
+            table[pl.ds(start, depth), :] = jnp.where(row == spots, 1.0, 0.0).astype(bf16)
+
+    hit = lax.broadcasted_iota(jnp.int32, (depth, size), 1) == col_ref[...]
+    diagonal_ref[...] = jnp.sum(jnp.where(hit, diagonal[...], 0.0), axis=1, keepdims=True)
+    picked = jnp.dot(
+        jnp.where(hit, 1.0, 0.0).astype(bf16), rest[...], preferred_element_type=f32
+    ).astype(bf16)
+    out_ref[...] = jnp.dot(picked, table[...], preferred_element_type=f32).astype(bf16)
+
+
+def slot_operator(dual_ops, row_perm, col_perm, sub):
+    size = dual_ops.shape[1]
+    depth = next(d for d in (256, 128, 64, 32, 16) if size % d == 0)
+    return pl.pallas_call(
+        setup_kernel,
+        grid=(1, size // depth),
+        out_shape=[
+            jax.ShapeDtypeStruct((size, size), bf16),
+            jax.ShapeDtypeStruct((size, 1), f32),
+        ],
+        in_specs=[
+            pl.BlockSpec((None, 1, size), lambda s, i: (sub, 0, 0)),
+            pl.BlockSpec((None, depth, 1), lambda s, i: (sub, i, 0)),
+            pl.BlockSpec((None, size, size), lambda s, i: (sub, 0, 0)),
+        ],
+        out_specs=[
+            pl.BlockSpec((depth, size), lambda s, i: (i, 0)),
+            pl.BlockSpec((depth, 1), lambda s, i: (i, 0)),
+        ],
+        scratch_shapes=[
+            pltpu.VMEM((size, size), bf16),
+            pltpu.VMEM((size, size), bf16),
+            pltpu.VMEM((1, size), f32),
+        ],
+        cost_estimate=pl.CostEstimate(
+            flops=4 * size**3, bytes_accessed=6 * size * size, transcendentals=0
+        ),
+        compiler_params=pltpu.CompilerParams(vmem_limit_bytes=56 * 2**20),
+    )(row_perm, col_perm, dual_ops)
+
+
+def apply_kernel(sub, d_ref, a_ref, lower_ref, upper_ref, lower_low_ref, upper_low_ref, xs):
+    half = a_ref.shape[0]
     step = pl.program_id(0)
-    depth, size = a_ref.shape[1:]
-    half = size // 2
 
     @pl.when(step == 0)
     def _():
         put_split(xs, pl.ds(0, half), -d_ref[sub])
         put_split(xs, pl.ds(half, half), d_ref[sub + 1])
-        spots = row_ref[...]
-
-        @pl.loop(0, size // depth)
-        def _(b):
-            start = pl.multiple_of(b * depth, depth)
-            want = lax.broadcasted_iota(jnp.int32, (depth, size), 0) + start
-            table = jnp.where(want == spots, 1.0, 0.0).astype(bf16)
-            xl[pl.ds(start, depth), :] = jnp.dot(
-                table, xs[...], preferred_element_type=f32
-            ).astype(bf16)
-
-    block = a_ref[0]
-    high = block.astype(bf16)
-    low = (block - high.astype(f32)).astype(bf16)
-    vector = xl[...]
-    pair = jnp.dot(high, vector, preferred_element_type=f32) + jnp.dot(
-        low, vector, preferred_element_type=f32
-    )
-    put_split(ys, pl.ds(pl.multiple_of(step * depth, depth), depth), joined_halves(pair))
-
-    @pl.when(step == size // depth - 1)
-    def _():
-        for side, out_ref in enumerate((lower_ref, upper_ref)):
-
-            @pl.loop(0, half // depth)
-            def _(b):
-                start = pl.multiple_of(b * depth, depth)
-                spots = col_ref[pl.ds(side * half + start, depth), :]
-                lane = lax.broadcasted_iota(jnp.int32, (depth, size), 1)
-                table = jnp.where(lane == spots, 1.0, 0.0).astype(bf16)
-                out_ref[pl.ds(start, depth), :] = joined_halves(
-                    jnp.dot(table, ys[...], preferred_element_type=f32)
+
+    outs = ((lower_ref, lower_low_ref), (upper_ref, upper_low_ref))
+    depth = half // 3 if half % 48 == 0 else half
+    for side, (wide, narrow) in enumerate(outs):
+
+        @pl.when(step == side)
+        def _():
+            for start in range(0, half, depth):
+                rows = pl.ds(start, depth)
+                value = joined_halves(
+                    jnp.dot(a_ref[rows, :], xs[...], preferred_element_type=f32)
                 )
-
-
-def apply_operator(direction, row_perm, col_perm, dual_ops, sub):
-    size = dual_ops.shape[1]
+                wide[rows, :] = value
+                narrow[rows, :] = value.astype(bf16)
+
+
+def apply_operator(direction, operator, sub):
+    size = operator.shape[0]
     half, width = direction.shape[1:]
-    depth = next(d for d in (256, 128, 64, 32, 16) if half % d == 0)
     return pl.pallas_call(
         functools.partial(apply_kernel, sub),
-        grid=(size // depth,),
-        out_shape=[jax.ShapeDtypeStruct((half, width), f32)] * 2,
+        grid=(2,),
+        out_shape=[jax.ShapeDtypeStruct((half, width), f32)] * 2
+        + [jax.ShapeDtypeStruct((half, width), bf16)] * 2,
         in_specs=[
             pl.BlockSpec(direction.shape, lambda i: (0, 0, 0)),
-            pl.BlockSpec((None, 1, size), lambda i: (sub, 0, 0)),
-            pl.BlockSpec((None, size, 1), lambda i: (sub, 0, 0)),
-            pl.BlockSpec((1, depth, size), lambda i: (sub, i, 0)),
-        ],
-        out_specs=[pl.BlockSpec((half, width), lambda i: (0, 0))] * 2,
-        scratch_shapes=[pltpu.VMEM((size, 2 * width), bf16)] * 3,
+            pl.BlockSpec((half, size), lambda i: (i, 0)),
+        ],
+        out_specs=[pl.BlockSpec((half, width), lambda i: (0, 0))] * 4,
+        scratch_shapes=[pltpu.VMEM((size, 2 * width), bf16)],
         cost_estimate=pl.CostEstimate(
-            flops=16 * size * size * width, bytes_accessed=4 * size * size, transcendentals=0
+            flops=4 * size * size * width, bytes_accessed=2 * size * size, transcendentals=0
         ),
-        compiler_params=pltpu.CompilerParams(vmem_limit_bytes=40 * 2**20),
-    )(direction, row_perm, col_perm, dual_ops)
+        compiler_params=pltpu.CompilerParams(vmem_limit_bytes=24 * 2**20),
+    )(direction, operator)
 
 
 def split(value, axis):
@@ -206,6 +241,15 @@
     live = (
         lax.broadcasted_iota(jnp.int32, (sub_count + 1, half_width), 1) < ext_size[:, None]
     ).astype(f32)[:, :, None]
+    operators, diagonals = zip(
+        *[slot_operator(dual_ops, row_view, col_view, sub) for sub in range(sub_count)]
+    )
+    upper_diagonals = [d[half_width:, 0] for d in diagonals]
+    lower_diagonals = [d[:half_width, 0] for d in diagonals]
+    upper_diagonals = [from_behind(upper_diagonals[-1], "dom", 1)] + upper_diagonals
+    lower_diagonals = lower_diagonals + [from_behind(lower_diagonals[0], "dom", -1)]
+    diagonal = jnp.stack(upper_diagonals) + jnp.stack(lower_diagonals)
+    diagonal = diagonal[:, :, None]
     column_table = (
         ext_cols[:, :, None] == lax.broadcasted_iota(jnp.int32, (1, 1, dom_count), 2)
     ).astype(f32)
@@ -247,10 +291,16 @@
         lowers, uppers = [None] * sub_count, [None] * sub_count
         order = [sub_count - 1] + list(range(sub_count - 1))
         for sub in order:
-            lowers[sub], uppers[sub] = apply_operator(direction, row_view, col_view, dual_ops, sub)
-        uppers = [from_behind(uppers[-1], "dom", 1)] + uppers
-        lowers = lowers + [from_behind(lowers[0], "dom", -1)]
-        mapped = jnp.stack([u - l for u, l in zip(uppers, lowers)]) * live
+            lower, upper, lower_low, upper_low = apply_operator(direction, operators[sub], sub)
+            lowers[sub], uppers[sub] = lower, upper
+            if sub == sub_count - 1:
+                rim_up = from_behind(upper_low, "dom", 1).astype(f32)
+            if sub == 0:
+                rim_low = from_behind(lower_low, "dom", -1).astype(f32)
+        uppers = [rim_up] + uppers
+        lowers = lowers + [rim_low]
+        rest = jnp.stack([u - l for u, l in zip(uppers, lowers)])
+        mapped = (diagonal * direction + rest) * live
         residual = residual - (mapped - correction_of(mapped))
         sums.append(jnp.sum(residual[1:] * residual[1:], axis=(0, 1)))
         if turn_index + 1 < STEPS:

time: 277 us -> 237 us (0.86)
  Pallas kernels: 149 us -> 120 us
  waiting for transfers between devices: 57.8 us -> 41.5 us
  local copies, waits for them, and re-layouts: 9.98 us -> 18.3 us
  other arithmetic: 20.4 us -> 16.9 us
    pallas_call x8 -> x10, Pallas kernels: 99.4 us -> 70.9 us  [the longest x2 52.5 us: slot_operator(): pl.pallas_call(setup_kernel, grid=(1, size // depth), out_shape=[jax.Shap...]
    ppermute x15 -> x17, waiting for transfers between devices: 57.8 us -> 41.5 us  [from_behind(): return lax.ppermute(block, axis, route)]
    unnamed x59 -> x109, local copies, waits for them, and re-layouts: 5.48 us -> 10.6 us
    slice x0 -> x2, local copies, waits for them, and re-layouts: none -> 2.84 us  [shards(): lower_diagonals = [d[:half_width, 0] for d in diagonals]]
    ppermute x15 -> x17, starting transfers between devices: 22.3 us -> 24.3 us  [from_behind(): return lax.ppermute(block, axis, route)]
  transfers between devices with their start and end apart: 15 -> 17, of which waited for: 6 -> 11; matrix products, arithmetic and copies ran while one was open for 6% -> 6% of each run, Pallas kernels for 7% -> 26%
where the time goes in v2:
time: 237 us; the launch traced here: 236 us
  Pallas kernels  120 us (51%)
  waiting for transfers between devices  41.5 us (18%)
  starting transfers between devices  24.3 us (10%)
  local copies, waits for them, and re-layouts  18.3 us (8%)
  other arithmetic  16.9 us (7%)
  matrix products  14.3 us (6%)
    pallas_call x2, Pallas kernels, slot_operator(): pl.pallas_call(setup_kernel, grid=(1, size // depth), out_shape=[jax.Shap...  52.5 us
    pallas_call x6, Pallas kernels, push_gather(): pl.pallas_call(functools.partial(gather_kernel, axes, sizes), out_shape=j...  48.6 us
    ppermute x17, waiting for transfers between devices, from_behind(): return lax.ppermute(block, axis, route)  41.5 us
    ppermute x17, starting transfers between devices, from_behind(): return lax.ppermute(block, axis, route)  24.3 us
    pallas_call x8, Pallas kernels, apply_operator(): pl.pallas_call(functools.partial(apply_kernel, sub), grid=(2,), out_shape...  18.4 us
    unnamed x109, local copies, waits for them, and re-layouts  10.6 us
    dot_general x5, matrix products, correction_of(): amounts = jnp.dot(coarse, everyone.astype(f32), precision=highest)  5.14 us
  transfers between devices with their start and end apart: 17, of which 11 were waited for; matrix products, arithmetic and copies ran while one was open for 6% of the time, Pallas kernels for 26%

profile of v2, /device:TPU:0, one launch (start us, length us, event | category | flops | bytes accessed | tf_op | source)
XLA Modules:
  0.0 236.4 jit_solution(8460805429323819744)
XLA Ops:
  2.2 3.0 %collective-permute-start.1 = (s32[9]{0:T(128)S(1)}, s32[9]{0:T(128)S(1)}, u32[]{:S(2)}, u32[]{:S(2)}) collective-permute-start(s32[9]{0:T(128)S(1)} %get-tuple-element.129), channel_id=1, source_target_pairs={{28,0},{0,4},{4,8},{8,12},{12,16},{16,20},{20,24},{24,28},{29,1},{... | collective-permute-start | bytes 116 | tf_op jit(solution)/shard_map/ppermute | solution.py:23
  5.2 3.1 %collective-permute-start.4 = (s32[9]{0:T(128)S(1)}, s32[9]{0:T(128)S(1)}, u32[]{:S(2)}, u32[]{:S(2)}) collective-permute-start(s32[9]{0:T(128)S(1)} %get-tuple-element.130), channel_id=1, source_target_pairs={{4,0},{8,4},{12,8},{16,12},{20,16},{24,20},{28,24},{0,28},{5,1},{9... | collective-permute-start | bytes 116 | tf_op jit(solution)/shard_map/ppermute | solution.py:23
  8.3 4.5 %fusion.3 = bf16[2,16,1536]{2,1,0:T(8,128)(2,1)S(1)} fusion(bf16[2,16,1536]{2,1,0:T(8,128)(2,1)S(1)} %copy-done, s32[2,1536]{1,0:T(2,128)} %param.13), kind=kOutput, calls=%fused_computation.4 | convolution fusion | flops 155762688 | bytes 208896 | tf_op jit(solution)/shard_map/sjn,skn->sjk/dot_general | solution.py:229
  12.8 2.0 collective-permute-start.3
  15.4 1.7 copy.19.col_ref
  17.1 26.2 %shard_map.104 = (bf16[1536,1536]{1,0:T(8,128)(2,1)}, f32[1536,1]{1,0:T(8,128)}) custom-call(s32[2,1,1536]{2,1,0:T(1,128)} %broadcast_in_dim.45.row_ref, s32[2,1536,1]{2,1,0:T(8,128)} %copy.19.col_ref, f32[2,1536,1536]{2,1,0:T(8,128)} %a_ref.3), custom_call_target="tpu_custom_call" | custom-call | flops 14495514624 | bytes 14155776 | tf_op jit(solution)/shard_map/pallas_call | solution.py:127
  46.2 26.3 %shard_map.103 = (bf16[1536,1536]{1,0:T(8,128)(2,1)}, f32[1536,1]{1,0:T(8,128)}) custom-call(s32[2,1,1536]{2,1,0:T(1,128)} %broadcast_in_dim.45.row_ref, s32[2,1536,1]{2,1,0:T(8,128)} %copy.19.col_ref, f32[2,1536,1536]{2,1,0:T(8,128)} %a_ref.3), custom_call_target="tpu_custom_call" | custom-call | flops 14495514624 | bytes 14155776 | tf_op jit(solution)/shard_map/pallas_call | solution.py:127
  77.5 4.5 %collective-permute-start.6 = (f32[8,16,16]{2,0,1:T(8,128)S(1)}, f32[8,16,16]{2,0,1:T(8,128)S(1)}, u32[]{:S(2)}, u32[]{:S(2)}) collective-permute-start(f32[8,16,16]{2,0,1:T(8,128)S(1)} %get-tuple-element.102), channel_id=1, source_target_pairs={{4,0},{8,4},{12,8},{16,12},{20,16},{24,20},{28,24},{0,28},{5,1},{9... | collective-permute-start | bytes 24584 | tf_op jit(solution)/shard_map/ppermute | solution.py:23
  84.6 8.9 %collective-permute-done = f32[768,128]{1,0:T(8,128)S(1)} collective-permute-done((f32[768,128]{1,0:T(8,128)S(1)}, f32[768,128]{1,0:T(8,128)S(1)}, u32[]{:S(2)}, u32[]{:S(2)}) %collective-permute-start) | collective-permute-done | bytes 393248 | tf_op jit(solution)/shard_map/ppermute | solution.py:23
  94.8 7.8 %shard_map.102 = bf16[8,2,16,128]{3,2,1,0:T(8,128)(2,1)} custom-call(bf16[2,16,128]{2,1,0:T(8,128)(2,1)} %fusion.89.x_ref), custom_call_target="tpu_custom_call" | custom-call | tf_op jit(solution)/shard_map/pallas_call | solution.py:72
  104.7 1.6 slice-done.1
  106.3 2.3 shard_map.106
  108.6 2.2 collective-permute-start.10
  110.8 2.3 shard_map.105
  114.3 7.2 %collective-permute-done.9 = bf16[768,128]{1,0:T(8,128)(2,1)S(1)} collective-permute-done((bf16[768,128]{1,0:T(8,128)(2,1)S(1)}, bf16[768,128]{1,0:T(8,128)(2,1)S(1)}, u32[]{:S(2)}, u32[]{:S(2)}) %collective-permute-start.9) | collective-permute-done | bytes 196640 | tf_op jit(solution)/shard_map/ppermute | solution.py:23
  124.1 7.8 %shard_map.107 = bf16[8,2,16,128]{3,2,1,0:T(8,128)(2,1)} custom-call(bf16[2,16,128]{2,1,0:T(8,128)(2,1)} %fusion.88.x_ref), custom_call_target="tpu_custom_call" | custom-call | tf_op jit(solution)/shard_map/pallas_call | solution.py:72
  135.4 2.3 shard_map.109
  137.7 2.3 shard_map.108
  142.3 3.4 %collective-permute-done.12 = bf16[768,128]{1,0:T(8,128)(2,1)S(1)} collective-permute-done((bf16[768,128]{1,0:T(8,128)(2,1)S(1)}, bf16[768,128]{1,0:T(8,128)(2,1)S(1)}, u32[]{:S(2)}, u32[]{:S(2)}) %collective-permute-start.12) | collective-permute-done | bytes 196640 | tf_op jit(solution)/shard_map/ppermute | solution.py:23
  145.7 4.0 %collective-permute-done.11 = bf16[768,128]{1,0:T(8,128)(2,1)S(1)} collective-permute-done((bf16[768,128]{1,0:T(8,128)(2,1)S(1)}, bf16[768,128]{1,0:T(8,128)(2,1)S(1)}, u32[]{:S(2)}, u32[]{:S(2)}) %collective-permute-start.11) | collective-permute-done | bytes 196640 | tf_op jit(solution)/shard_map/ppermute | solution.py:23
  152.5 7.8 %shard_map.110 = bf16[8,2,16,128]{3,2,1,0:T(8,128)(2,1)} custom-call(bf16[2,16,128]{2,1,0:T(8,128)(2,1)} %fusion.87.x_ref), custom_call_target="tpu_custom_call" | custom-call | tf_op jit(solution)/shard_map/pallas_call | solution.py:72
  164.6 2.3 shard_map.112
  166.9 2.3 shard_map.111
  171.5 3.5 %collective-permute-done.14 = bf16[768,128]{1,0:T(8,128)(2,1)S(1)} collective-permute-done((bf16[768,128]{1,0:T(8,128)(2,1)S(1)}, bf16[768,128]{1,0:T(8,128)(2,1)S(1)}, u32[]{:S(2)}, u32[]{:S(2)}) %collective-permute-start.14) | collective-permute-done | bytes 196640 | tf_op jit(solution)/shard_map/ppermute | solution.py:23
  174.9 4.3 %collective-permute-done.13 = bf16[768,128]{1,0:T(8,128)(2,1)S(1)} collective-permute-done((bf16[768,128]{1,0:T(8,128)(2,1)S(1)}, bf16[768,128]{1,0:T(8,128)(2,1)S(1)}, u32[]{:S(2)}, u32[]{:S(2)}) %collective-permute-start.13) | collective-permute-done | bytes 196640 | tf_op jit(solution)/shard_map/ppermute | solution.py:23
  182.1 7.8 %shard_map.113 = bf16[8,2,16,128]{3,2,1,0:T(8,128)(2,1)} custom-call(bf16[2,16,128]{2,1,0:T(8,128)(2,1)} %fusion.86.x_ref), custom_call_target="tpu_custom_call" | custom-call | tf_op jit(solution)/shard_map/pallas_call | solution.py:72
  194.3 2.3 shard_map.115
  196.6 2.3 shard_map.114
  202.1 3.8 %collective-permute-done.16 = bf16[768,128]{1,0:T(8,128)(2,1)S(1)} collective-permute-done((bf16[768,128]{1,0:T(8,128)(2,1)S(1)}, bf16[768,128]{1,0:T(8,128)(2,1)S(1)}, u32[]{:S(2)}, u32[]{:S(2)}) %collective-permute-start.16) | collective-permute-done | bytes 196640 | tf_op jit(solution)/shard_map/ppermute | solution.py:23
  205.9 3.6 %collective-permute-done.15 = bf16[768,128]{1,0:T(8,128)(2,1)S(1)} collective-permute-done((bf16[768,128]{1,0:T(8,128)(2,1)S(1)}, bf16[768,128]{1,0:T(8,128)(2,1)S(1)}, u32[]{:S(2)}, u32[]{:S(2)}) %collective-permute-start.15) | collective-permute-done | bytes 196640 | tf_op jit(solution)/shard_map/ppermute | solution.py:23
  212.2 7.8 %shard_map.116 = bf16[8,2,16,128]{3,2,1,0:T(8,128)(2,1)} custom-call(bf16[2,16,128]{2,1,0:T(8,128)(2,1)} %fusion.85.x_ref), custom_call_target="tpu_custom_call" | custom-call | tf_op jit(solution)/shard_map/pallas_call | solution.py:72
  224.7 9.6 %shard_map.117 = f32[32,8,128]{2,1,0:T(8,128)} custom-call(f32[8,128]{1,0:T(8,128)} %select_maximum_fusion.x_ref), custom_call_target="tpu_custom_call" | custom-call | tf_op jit(solution)/shard_map/pallas_call | solution.py:72
  (227 shorter events, 54.2 us)
Async XLA Ops:
  2.2 73.0 %collective-permute-start.1 = (s32[9]{0:T(128)S(1)}, s32[9]{0:T(128)S(1)}, u32[]{:S(2)}, u32[]{:S(2)}) collective-permute-start(s32[9]{0:T(128)S(1)} %get-tuple-element.129), channel_id=1, source_target_pairs={{28,0},{0,4},{4,8},{8,12},{12,16},{16,20},{20,24},{24,28},{29,1},{... | collective-permute-start | bytes 116 | tf_op jit(solution)/shard_map/ppermute | solution.py:23
  5.2 9.7 %copy-start.24 = (s32[2,1536]{1,0:T(2,128)S(1)}, s32[2,1536]{1,0:T(2,128)}, u32[]{:S(2)}) copy-start(s32[2,1536]{1,0:T(2,128)} %param.13) | copy-start | bytes 36868
  5.2 71.3 %collective-permute-start.4 = (s32[9]{0:T(128)S(1)}, s32[9]{0:T(128)S(1)}, u32[]{:S(2)}, u32[]{:S(2)}) collective-permute-start(s32[9]{0:T(128)S(1)} %get-tuple-element.130), channel_id=1, source_target_pairs={{4,0},{8,4},{12,8},{16,12},{20,16},{24,20},{28,24},{0,28},{5,1},{9... | collective-permute-start | bytes 116 | tf_op jit(solution)/shard_map/ppermute | solution.py:23
  12.8 71.8 %collective-permute-start.3 = (bf16[16,1536]{1,0:T(8,128)(2,1)S(1)}, bf16[16,1536]{1,0:T(8,128)(2,1)S(1)}, u32[]{:S(2)}, u32[]{:S(2)}) collective-permute-start(bf16[16,1536]{1,0:T(8,128)(2,1)S(1)} %get-tuple-element.103), channel_id=1, source_target_pairs={{4,0},{8,4},{12,8},{16,12},{20,16},{24,20},{28,24},{0,28},{5,1},{9... | collective-permute-start | bytes 147464 | tf_op jit(solution)/shard_map/ppermute | solution.py:23
  44.7 29.9 %copy-start.37 = (s32[2]{0:T(128)S(1)}, s32[2]{0:T(128)}, u32[]{:S(2)}) copy-start(s32[2]{0:T(128)} %param.14) | copy-start | bytes 28
  44.7 30.0 %copy-start.23 = (f32[2,8,16,16]{3,2,1,0:T(8,128)S(1)}, f32[2,8,16,16]{3,2,1,0:T(8,128)}, u32[]{:S(2)}) copy-start(f32[2,8,16,16]{3,2,1,0:T(8,128)} %param.11) | copy-start | bytes 49156
  44.7 32.7 %collective-permute-start.8 = (f32[768]{0:T(1024)S(1)}, f32[768]{0:T(1024)S(1)}, u32[]{:S(2)}, u32[]{:S(2)}) collective-permute-start(f32[768]{0:T(1024)S(1)} %get-tuple-element.74), channel_id=1, source_target_pairs={{4,0},{8,4},{12,8},{16,12},{20,16},{24,20},{28,24},{0,28},{5,1},{9... | collective-permute-start | bytes 9224 | tf_op jit(solution)/shard_map/ppermute | solution.py:23
  73.9 8.0 %collective-permute-start.7 = (f32[768]{0:T(1024)S(1)}, f32[768]{0:T(1024)S(1)}, u32[]{:S(2)}, u32[]{:S(2)}) collective-permute-start(f32[768]{0:T(1024)S(1)} %get-tuple-element.73), channel_id=1, source_target_pairs={{28,0},{0,4},{4,8},{8,12},{12,16},{16,20},{20,24},{24,28},{29,1},{... | collective-permute-start | bytes 9224 | tf_op jit(solution)/shard_map/ppermute | solution.py:23
  74.7 19.1 %copy-start.25 = (bf16[2,16,768]{2,1,0:T(8,128)(2,1)}, bf16[2,16,768]{2,1,0:T(8,128)(2,1)S(1)}, u32[]{:S(2)}) copy-start(bf16[2,16,768]{2,1,0:T(8,128)(2,1)S(1)} %get-tuple-element.105) | copy-start | bytes 147460
  74.7 19.1 %copy-start.30 = (bf16[2,16,768]{2,1,0:T(8,128)(2,1)}, bf16[2,16,768]{2,1,0:T(8,128)(2,1)S(1)}, u32[]{:S(2)}) copy-start(bf16[2,16,768]{2,1,0:T(8,128)(2,1)S(1)} %get-tuple-element.106) | copy-start | bytes 147460
  75.2 28.5 %collective-permute-start.2 = (bf16[16,1536]{1,0:T(8,128)(2,1)S(1)}, bf16[16,1536]{1,0:T(8,128)(2,1)S(1)}, u32[]{:S(2)}, u32[]{:S(2)}) collective-permute-start(bf16[16,1536]{1,0:T(8,128)(2,1)S(1)} %get-tuple-element.104), channel_id=1, source_target_pairs={{28,0},{0,4},{4,8},{8,12},{12,16},{16,20},{20,24},{24,28},{29,1},{... | collective-permute-start | bytes 147464 | tf_op jit(solution)/shard_map/ppermute | solution.py:23
  76.5 7.0 %collective-permute-start.5 = (f32[8,16,16]{2,0,1:T(8,128)S(1)}, f32[8,16,16]{2,0,1:T(8,128)S(1)}, u32[]{:S(2)}, u32[]{:S(2)}) collective-permute-start(f32[8,16,16]{2,0,1:T(8,128)S(1)} %get-tuple-element.101), channel_id=1, source_target_pairs={{28,0},{0,4},{4,8},{8,12},{12,16},{16,20},{20,24},{24,28},{29,1},{... | collective-permute-start | bytes 24584 | tf_op jit(solution)/shard_map/ppermute | solution.py:23
  77.5 6.4 %collective-permute-start.6 = (f32[8,16,16]{2,0,1:T(8,128)S(1)}, f32[8,16,16]{2,0,1:T(8,128)S(1)}, u32[]{:S(2)}, u32[]{:S(2)}) collective-permute-start(f32[8,16,16]{2,0,1:T(8,128)S(1)} %get-tuple-element.102), channel_id=1, source_target_pairs={{4,0},{8,4},{12,8},{16,12},{20,16},{24,20},{28,24},{0,28},{5,1},{9... | collective-permute-start | bytes 24584 | tf_op jit(solution)/shard_map/ppermute | solution.py:23
  81.9 11.6 %collective-permute-start = (f32[768,128]{1,0:T(8,128)S(1)}, f32[768,128]{1,0:T(8,128)S(1)}, u32[]{:S(2)}, u32[]{:S(2)}) collective-permute-start(f32[768,128]{1,0:T(8,128)S(1)} %slice_bitcast_fusion), channel_id=1, source_target_pairs={{28,0},{0,4},{4,8},{8,12},{12,16},{16,20},{20,24},{24,28},{29,1},{... | collective-permute-start | bytes 1179656 | tf_op jit(solution)/shard_map/ppermute | solution.py:23
  93.8 10.8 %slice-start = ((s8[4718592]{0:T(1024)(128)(4,1)}), s8[524288]{0:T(1024)(128)(4,1)S(1)}, s32[]{:S(2)}) async-start(s8[4718592]{0:T(1024)(128)(4,1)} %bitcast.92), calls=%async_computation | async-start | bytes 1048576
  108.6 5.7 %collective-permute-start.10 = (bf16[768,128]{1,0:T(8,128)(2,1)S(1)}, bf16[768,128]{1,0:T(8,128)(2,1)S(1)}, u32[]{:S(2)}, u32[]{:S(2)}) collective-permute-start(bf16[768,128]{1,0:T(8,128)(2,1)S(1)} %get-tuple-element.53), channel_id=1, source_target_pairs={{4,0},{8,4},{12,8},{16,12},{20,16},{24,20},{28,24},{0,28},{5,1},{9... | collective-permute-start | bytes 589832 | tf_op jit(solution)/shard_map/ppermute | solution.py:23
  113.1 8.4 %collective-permute-start.9 = (bf16[768,128]{1,0:T(8,128)(2,1)S(1)}, bf16[768,128]{1,0:T(8,128)(2,1)S(1)}, u32[]{:S(2)}, u32[]{:S(2)}) collective-permute-start(bf16[768,128]{1,0:T(8,128)(2,1)S(1)} %get-tuple-element.47), channel_id=1, source_target_pairs={{28,0},{0,4},{4,8},{8,12},{12,16},{16,20},{20,24},{24,28},{29,1},{... | collective-permute-start | bytes 589832 | tf_op jit(solution)/shard_map/ppermute | solution.py:23
  123.2 9.8 %copy-start.18 = (bf16[16,1536]{1,0:T(8,128)(2,1)S(1)}, bf16[16,1536]{1,0:T(8,128)(2,1)}, u32[]{:S(2)}) copy-start(bf16[16,1536]{1,0:T(8,128)(2,1)} %copy-done.17) | copy-start | bytes 147460
  123.2 11.7 %slice-start.2 = ((s8[4718592]{0:T(1024)(128)(4,1)}), s8[524288]{0:T(1024)(128)(4,1)S(1)}, s32[]{:S(2)}) async-start(s8[4718592]{0:T(1024)(128)(4,1)} %bitcast.94), calls=%async_computation.2 | async-start | bytes 1048576
  140.0 5.7 %collective-permute-start.12 = (bf16[768,128]{1,0:T(8,128)(2,1)S(1)}, bf16[768,128]{1,0:T(8,128)(2,1)S(1)}, u32[]{:S(2)}, u32[]{:S(2)}) collective-permute-start(bf16[768,128]{1,0:T(8,128)(2,1)S(1)} %get-tuple-element.59), channel_id=1, source_target_pairs={{4,0},{8,4},{12,8},{16,12},{20,16},{24,20},{28,24},{0,28},{5,1},{9... | collective-permute-start | bytes 589832 | tf_op jit(solution)/shard_map/ppermute | solution.py:23
  141.1 8.5 %collective-permute-start.11 = (bf16[768,128]{1,0:T(8,128)(2,1)S(1)}, bf16[768,128]{1,0:T(8,128)(2,1)S(1)}, u32[]{:S(2)}, u32[]{:S(2)}) collective-permute-start(bf16[768,128]{1,0:T(8,128)(2,1)S(1)} %get-tuple-element.54), channel_id=1, source_target_pairs={{28,0},{0,4},{4,8},{8,12},{12,16},{16,20},{20,24},{24,28},{29,1},{... | collective-permute-start | bytes 589832 | tf_op jit(solution)/shard_map/ppermute | solution.py:23
  151.6 9.9 %copy-start.19 = (bf16[16,1536]{1,0:T(8,128)(2,1)S(1)}, bf16[16,1536]{1,0:T(8,128)(2,1)}, u32[]{:S(2)}) copy-start(bf16[16,1536]{1,0:T(8,128)(2,1)} %copy-done.17) | copy-start | bytes 147460
  151.6 15.3 %slice-start.12 = ((s8[4718592]{0:T(1024)(128)(4,1)}), s8[524288]{0:T(1024)(128)(4,1)S(1)}, s32[]{:S(2)}) async-start(s8[4718592]{0:T(1024)(128)(4,1)} %bitcast.104), calls=%async_computation.12 | async-start | bytes 1048576
  163.2 8.1 %copy-start.8 = (f32[3,768,128]{2,1,0:T(8,128)}, f32[3,768,128]{2,1,0:T(8,128)S(1)}, u32[]{:S(2)}) copy-start(f32[3,768,128]{2,1,0:T(8,128)S(1)} %get-tuple-element.85) | copy-start | bytes 3538948
  169.2 5.8 %collective-permute-start.14 = (bf16[768,128]{1,0:T(8,128)(2,1)S(1)}, bf16[768,128]{1,0:T(8,128)(2,1)S(1)}, u32[]{:S(2)}, u32[]{:S(2)}) collective-permute-start(bf16[768,128]{1,0:T(8,128)(2,1)S(1)} %get-tuple-element.65), channel_id=1, source_target_pairs={{4,0},{8,4},{12,8},{16,12},{20,16},{24,20},{28,24},{0,28},{5,1},{9... | collective-permute-start | bytes 589832 | tf_op jit(solution)/shard_map/ppermute | solution.py:23
  170.3 8.9 %collective-permute-start.13 = (bf16[768,128]{1,0:T(8,128)(2,1)S(1)}, bf16[768,128]{1,0:T(8,128)(2,1)S(1)}, u32[]{:S(2)}, u32[]{:S(2)}) collective-permute-start(bf16[768,128]{1,0:T(8,128)(2,1)S(1)} %get-tuple-element.60), channel_id=1, source_target_pairs={{28,0},{0,4},{4,8},{8,12},{12,16},{16,20},{20,24},{24,28},{29,1},{... | collective-permute-start | bytes 589832 | tf_op jit(solution)/shard_map/ppermute | solution.py:23
  181.1 9.8 %copy-start.20 = (bf16[16,1536]{1,0:T(8,128)(2,1)S(1)}, bf16[16,1536]{1,0:T(8,128)(2,1)}, u32[]{:S(2)}) copy-start(bf16[16,1536]{1,0:T(8,128)(2,1)} %copy-done.17) | copy-start | bytes 147460
  181.1 15.5 %slice-start.14 = ((s8[4718592]{0:T(1024)(128)(4,1)}), s8[524288]{0:T(1024)(128)(4,1)S(1)}, s32[]{:S(2)}) async-start(s8[4718592]{0:T(1024)(128)(4,1)} %bitcast.106), calls=%async_computation.14 | async-start | bytes 1048576
  200.0 5.8 %collective-permute-start.16 = (bf16[768,128]{1,0:T(8,128)(2,1)S(1)}, bf16[768,128]{1,0:T(8,128)(2,1)S(1)}, u32[]{:S(2)}, u32[]{:S(2)}) collective-permute-start(bf16[768,128]{1,0:T(8,128)(2,1)S(1)} %get-tuple-element.71), channel_id=1, source_target_pairs={{4,0},{8,4},{12,8},{16,12},{20,16},{24,20},{28,24},{0,28},{5,1},{9... | collective-permute-start | bytes 589832 | tf_op jit(solution)/shard_map/ppermute | solution.py:23
  201.2 8.4 %collective-permute-start.15 = (bf16[768,128]{1,0:T(8,128)(2,1)S(1)}, bf16[768,128]{1,0:T(8,128)(2,1)S(1)}, u32[]{:S(2)}, u32[]{:S(2)}) collective-permute-start(bf16[768,128]{1,0:T(8,128)(2,1)S(1)} %get-tuple-element.66), channel_id=1, source_target_pairs={{28,0},{0,4},{4,8},{8,12},{12,16},{16,20},{20,24},{24,28},{29,1},{... | collective-permute-start | bytes 589832 | tf_op jit(solution)/shard_map/ppermute | solution.py:23
  211.3 9.8 %copy-start.21 = (bf16[16,1536]{1,0:T(8,128)(2,1)S(1)}, bf16[16,1536]{1,0:T(8,128)(2,1)}, u32[]{:S(2)}) copy-start(bf16[16,1536]{1,0:T(8,128)(2,1)} %copy-done.17) | copy-start | bytes 147460
  221.8 14.6 %copy-start.1 = (bf16[2,16,1536]{2,1,0:T(8,128)(2,1)S(1)}, bf16[2,16,1536]{2,1,0:T(8,128)(2,1)}, u32[]{:S(2)}) copy-start(bf16[2,16,1536]{2,1,0:T(8,128)(2,1)} %param.10) | copy-start | bytes 294916
  (39 other events, 100.2 us)

commit v3 on v2

--- a/solution.py
+++ b/solution.py
@@ -81,6 +81,77 @@
         ],
         compiler_params=pltpu.CompilerParams(collective_id=collective_id, has_side_effects=True),
     )(block)
+
+
+def exchange_kernel(
+    count, part_ref, share_ref, up_ref, low_ref, all_ref, up_in, low_in, shares,
+    share_send, share_recv, rim_send, rim_recv, send_sem, recv_sem
+):
+    me = lax.axis_index("dom")
+    others = [{"dom": lax.rem(me + k, count)} for k in range(1, count)]
+    barrier = pltpu.get_barrier_semaphore()
+    for target in others:
+        pl.semaphore_signal(
+            barrier, inc=1, device_id=target, device_id_type=pl.DeviceIdType.MESH
+        )
+    pl.semaphore_wait(barrier, count - 1)
+
+    def send(source, destination, send_at, recv_at, target):
+        copy = pltpu.make_async_remote_copy(
+            src_ref=source,
+            dst_ref=destination,
+            send_sem=send_at,
+            recv_sem=recv_at,
+            device_id=target,
+            device_id_type=pl.DeviceIdType.MESH,
+        )
+        copy.start()
+        return copy
+
+    ends = (others[0], others[-1])
+    first = [
+        send(share_ref.at[k], shares.at[k], share_send.at[k], share_recv.at[k], ends[k])
+        for k in range(2)
+    ]
+    rims = [
+        send(source, destination, rim_send.at[k], rim_recv.at[k], ends[k])
+        for k, (source, destination) in enumerate(((up_ref, up_in), (low_ref, low_in)))
+    ]
+    for copy in first:
+        copy.wait()
+    subs = part_ref.shape[0]
+    for sub in range(subs):
+        value = part_ref[sub]
+        if sub == 0:
+            value = value + shares[0]
+        if sub == subs - 1:
+            value = value + shares[1]
+        all_ref[me, sub] = value.astype(bf16)
+    pushes = [
+        send(all_ref.at[me], all_ref.at[me], send_sem.at[k], recv_sem.at[k], target)
+        for k, target in enumerate(others)
+    ]
+    for copy in pushes + rims:
+        copy.wait()
+
+
+def exchange(part, share, up, low, collective_id):
+    count = lax.axis_size("dom")
+    vmem = pl.BlockSpec(memory_space=pltpu.VMEM)
+    return pl.pallas_call(
+        functools.partial(exchange_kernel, count),
+        out_shape=[
+            jax.ShapeDtypeStruct((count,) + part.shape, bf16),
+            jax.ShapeDtypeStruct(up.shape, up.dtype),
+            jax.ShapeDtypeStruct(low.shape, low.dtype),
+        ],
+        in_specs=[vmem] * 4,
+        out_specs=[vmem] * 3,
+        scratch_shapes=[pltpu.VMEM(share.shape, f32)]
+        + [pltpu.SemaphoreType.DMA((2,))] * 4
+        + [pltpu.SemaphoreType.DMA((count - 1,))] * 2,
+        compiler_params=pltpu.CompilerParams(collective_id=collective_id, has_side_effects=True),
+    )(part, share, up, low)
 
 
 def put_split(ref, rows, value):
@@ -261,15 +332,15 @@
         [ext_modes[:-1, :, half_width:], -ext_modes[1:, :, :half_width]], axis=1
     )
 
-    def correction_of(vector):
+    def fit(vector):
         pairs = split(vector, 2)
         locals_ = jnp.concatenate([pairs[:-1], pairs[1:]], axis=1)
-        coefficients = unsplit(
-            jnp.einsum("sjn,snc->sjc", fit_modes, locals_, preferred_element_type=f32)
-        ).astype(bf16)
-        everyone = push_gather(coefficients, ("dom",), 1).reshape(
-            dom_count * mode_count, case_count
-        )
+        return unsplit(jnp.einsum("sjn,snc->sjc", fit_modes, locals_, preferred_element_type=f32))
+
+    share_modes = jnp.stack([-ext_modes[-1, :, :half_width], -ext_modes[0, :, half_width:]])
+
+    def correction_of(everyone):
+        everyone = everyone.reshape(dom_count * mode_count, case_count)
         amounts = jnp.dot(coarse, everyone.astype(f32), precision=highest)
         amounts = split(amounts, 1).reshape(sub_count + 2, mode_count, 2 * case_count)
         amounts = jnp.concatenate([amounts[:-1], amounts[1:]], axis=1)
@@ -282,7 +353,7 @@
     spread_ratio = centre / radius
     ratio_now = 1.0 / spread_ratio
     residual = jnp.concatenate([prior_rim[None], start_vector], axis=0)
-    residual = residual - correction_of(residual)
+    residual = residual - correction_of(push_gather(fit(residual).astype(bf16), ("dom",), 1))
     direction = residual / centre
     solution = jnp.zeros_like(rhs)
     sums = []
@@ -294,14 +365,20 @@
             lower, upper, lower_low, upper_low = apply_operator(direction, operators[sub], sub)
             lowers[sub], uppers[sub] = lower, upper
             if sub == sub_count - 1:
-                rim_up = from_behind(upper_low, "dom", 1).astype(f32)
+                up_low = upper_low
             if sub == 0:
-                rim_low = from_behind(lower_low, "dom", -1).astype(f32)
-        uppers = [rim_up] + uppers
-        lowers = lowers + [rim_low]
-        rest = jnp.stack([u - l for u, l in zip(uppers, lowers)])
+                low_low = lower_low
+        none = jnp.zeros_like(lowers[0])
+        rest = jnp.stack([u - l for u, l in zip([none] + uppers, lowers + [none])])
         mapped = (diagonal * direction + rest) * live
-        residual = residual - (mapped - correction_of(mapped))
+        ends = jnp.stack([uppers[-1] * live[-1], lowers[0] * live[0]])
+        share = unsplit(
+            jnp.einsum("sjn,snc->sjc", share_modes, split(ends, 2), preferred_element_type=f32)
+        )
+        everyone, rim_up, rim_low = exchange(fit(mapped), share, up_low, low_low, 3)
+        mapped = mapped.at[0].add(rim_up.astype(f32) * live[0])
+        mapped = mapped.at[-1].add(-rim_low.astype(f32) * live[-1])
+        residual = residual - (mapped - correction_of(everyone))
         sums.append(jnp.sum(residual[1:] * residual[1:], axis=(0, 1)))
         if turn_index + 1 < STEPS:
             ratio_next = 1.0 / (2.0 * spread_ratio - ratio_now)

time: 237 us -> 234 us (0.987)
  waiting for transfers between devices: 41.5 us -> 10.8 us
  Pallas kernels: 120 us -> 139 us
  other arithmetic: 16.9 us -> 35.2 us
  starting transfers between devices: 24.3 us -> 16.1 us
  local copies, waits for them, and re-layouts: 18.3 us -> 15.4 us
    pallas_call x0 -> x4, Pallas kernels: none -> 50.9 us  [exchange(): pl.pallas_call(functools.partial(exchange_kernel, count), out_shape=[jax....]
    pallas_call x6 -> x2, Pallas kernels: 48.6 us -> 17.4 us  [push_gather(): pl.pallas_call(functools.partial(gather_kernel, axes, sizes), out_shape=j...]
    ppermute x17 -> x9, waiting for transfers between devices: 41.5 us -> 10.8 us  [from_behind(): return lax.ppermute(block, axis, route)]
    scatter-add x0 -> x8, other arithmetic: none -> 10.8 us  [the longest x4 6.54 us: shards(): mapped = mapped.at[0].add(rim_up.astype(f32) * live[0])]
    ppermute x17 -> x9, starting transfers between devices: 24.3 us -> 16.1 us  [from_behind(): return lax.ppermute(block, axis, route)]
    add x0 -> x8, other arithmetic: none -> 4.86 us  [unsplit(): return pair[..., :width] + pair[..., width:]]
    add x3, other arithmetic: 2.63 us -> 6.09 us  [shards(): ratio_next * ratio_now * direction + 2.0 * ratio_next / radius * residual]
    convert_element_type x5 -> x1, other arithmetic: 3.05 us -> 0.61 us  [shards(): fit(residual).astype(bf16)]
  transfers between devices with their start and end apart: 17 -> 9, of which waited for: 11 -> 2; matrix products, arithmetic and copies ran while one was open for 6% -> 5% of each run, Pallas kernels for 26% -> 22%
where the time goes in v3:
time: 234 us
  Pallas kernels  139 us (59%)
  other arithmetic  35.2 us (15%)
  starting transfers between devices  16.1 us (7%)
  local copies, waits for them, and re-layouts  15.4 us (7%)
  matrix products  15.1 us (6%)
  waiting for transfers between devices  10.8 us (5%)
    pallas_call x2, Pallas kernels, slot_operator(): pl.pallas_call(setup_kernel, grid=(1, size // depth), out_shape=[jax.Shap...  52.5 us
    pallas_call x4, Pallas kernels, exchange(): pl.pallas_call(functools.partial(exchange_kernel, count), out_shape=[jax....  50.9 us
    pallas_call x8, Pallas kernels, apply_operator(): pl.pallas_call(functools.partial(apply_kernel, sub), grid=(2,), out_shape...  18.7 us
    pallas_call x2, Pallas kernels, push_gather(): pl.pallas_call(functools.partial(gather_kernel, axes, sizes), out_shape=j...  17.4 us
    ppermute x9, starting transfers between devices, from_behind(): return lax.ppermute(block, axis, route)  16.1 us
    ppermute x9, waiting for transfers between devices, from_behind(): return lax.ppermute(block, axis, route)  10.8 us
    unnamed x89, local copies, waits for them, and re-layouts  8.25 us
    scatter-add x4, other arithmetic, shards(): mapped = mapped.at[0].add(rim_up.astype(f32) * live[0])  6.54 us
  transfers between devices with their start and end apart: 9, of which 2 were waited for; matrix products, arithmetic and copies ran while one was open for 5% of the time, Pallas kernels for 22%

profile of v3, /device:TPU:0, one launch (start us, length us, event | category | flops | bytes accessed | tf_op | source)
XLA Modules:
  0.0 233.5 jit_solution(8307408562344481184)
XLA Ops:
  2.2 3.0 %collective-permute-start.1 = (s32[9]{0:T(128)S(1)}, s32[9]{0:T(128)S(1)}, u32[]{:S(2)}, u32[]{:S(2)}) collective-permute-start(s32[9]{0:T(128)S(1)} %get-tuple-element.267), channel_id=1, source_target_pairs={{28,0},{0,4},{4,8},{8,12},{12,16},{16,20},{20,24},{24,28},{29,1},{... | collective-permute-start | bytes 116 | tf_op jit(solution)/shard_map/ppermute | solution.py:23
  5.2 3.1 %collective-permute-start.4 = (s32[9]{0:T(128)S(1)}, s32[9]{0:T(128)S(1)}, u32[]{:S(2)}, u32[]{:S(2)}) collective-permute-start(s32[9]{0:T(128)S(1)} %get-tuple-element.268), channel_id=1, source_target_pairs={{4,0},{8,4},{12,8},{16,12},{20,16},{24,20},{28,24},{0,28},{5,1},{9... | collective-permute-start | bytes 116 | tf_op jit(solution)/shard_map/ppermute | solution.py:23
  8.3 4.5 %fusion.3 = bf16[2,16,1536]{2,1,0:T(8,128)(2,1)S(1)} fusion(bf16[2,16,1536]{2,1,0:T(8,128)(2,1)S(1)} %copy-done, s32[2,1536]{1,0:T(2,128)} %param.29), kind=kOutput, calls=%fused_computation.4 | convolution fusion | flops 155762688 | bytes 208896 | tf_op jit(solution)/shard_map/sjn,skn->sjk/dot_general | solution.py:300
  12.8 2.0 collective-permute-start.3
  15.4 1.6 copy.19.col_ref
  17.1 26.2 %shard_map.104 = (bf16[1536,1536]{1,0:T(8,128)(2,1)}, f32[1536,1]{1,0:T(8,128)}) custom-call(s32[2,1,1536]{2,1,0:T(1,128)} %broadcast_in_dim.45.row_ref, s32[2,1536,1]{2,1,0:T(8,128)} %copy.19.col_ref, f32[2,1536,1536]{2,1,0:T(8,128)} %a_ref.3), custom_call_target="tpu_custom_call" | custom-call | flops 14495514624 | bytes 14155776 | tf_op jit(solution)/shard_map/pallas_call | solution.py:198
  44.7 1.5 collective-permute-start.8
  46.2 26.2 %shard_map.103 = (bf16[1536,1536]{1,0:T(8,128)(2,1)}, f32[1536,1]{1,0:T(8,128)}) custom-call(s32[2,1,1536]{2,1,0:T(1,128)} %broadcast_in_dim.45.row_ref, s32[2,1536,1]{2,1,0:T(8,128)} %copy.19.col_ref, f32[2,1536,1536]{2,1,0:T(8,128)} %a_ref.3), custom_call_target="tpu_custom_call" | custom-call | flops 14495514624 | bytes 14155776 | tf_op jit(solution)/shard_map/pallas_call | solution.py:198
  76.9 4.5 %collective-permute-start.6 = (f32[8,16,16]{2,0,1:T(8,128)S(1)}, f32[8,16,16]{2,0,1:T(8,128)S(1)}, u32[]{:S(2)}, u32[]{:S(2)}) collective-permute-start(f32[8,16,16]{2,0,1:T(8,128)S(1)} %get-tuple-element.240), channel_id=1, source_target_pairs={{4,0},{8,4},{12,8},{16,12},{20,16},{24,20},{28,24},{0,28},{5,1},{9... | collective-permute-start | bytes 24584 | tf_op jit(solution)/shard_map/ppermute | solution.py:23
  81.5 2.0 collective-permute-done.5
  84.3 8.7 %collective-permute-done = f32[768,128]{1,0:T(8,128)S(1)} collective-permute-done((f32[768,128]{1,0:T(8,128)S(1)}, f32[768,128]{1,0:T(8,128)S(1)}, u32[]{:S(2)}, u32[]{:S(2)}) %collective-permute-start) | collective-permute-done | bytes 393248 | tf_op jit(solution)/shard_map/ppermute | solution.py:23
  94.2 7.8 %shard_map.102 = bf16[8,2,16,128]{3,2,1,0:T(8,128)(2,1)} custom-call(bf16[2,16,128]{2,1,0:T(8,128)(2,1)} %fusion.113.x_ref), custom_call_target="tpu_custom_call" | custom-call | tf_op jit(solution)/shard_map/pallas_call | solution.py:72
  104.1 2.0 slice-done.1
  106.1 2.3 shard_map.105
  109.1 2.3 shard_map.106
  115.0 12.6 %shard_map.107 = (bf16[8,2,16,128]{3,2,1,0:T(8,128)(2,1)}, bf16[768,128]{1,0:T(8,128)(2,1)}, bf16[768,128]{1,0:T(8,128)(2,1)}) custom-call(f32[2,16,128]{2,1,0:T(8,128)} %slice_add_fusion.23.part_ref, f32[2,16,128]{2,1,0:T(8,128)} %slice_add_fusion.22.share_ref, bf16[768,128]{1,0:T(8,128)(2,1)} %copy-done.9, bf16[768,128]{1,0:T(8,128)(2,1)} %copy-done.6), custom_call_target="tpu_custom_call" | custom-call | tf_op jit(solution)/shard_map/pallas_call | solution.py:141
  132.1 2.3 shard_map.109
  135.1 2.3 shard_map.108
  141.4 12.8 %shard_map.110 = (bf16[8,2,16,128]{3,2,1,0:T(8,128)(2,1)}, bf16[768,128]{1,0:T(8,128)(2,1)}, bf16[768,128]{1,0:T(8,128)(2,1)}) custom-call(f32[2,16,128]{2,1,0:T(8,128)} %slice_add_fusion.21.part_ref, f32[2,16,128]{2,1,0:T(8,128)} %slice_add_fusion.20.share_ref, bf16[768,128]{1,0:T(8,128)(2,1)} %copy-done.7, bf16[768,128]{1,0:T(8,128)(2,1)} %copy-done.10), custom_call_target="tpu_custom_call" | custom-call | tf_op jit(solution)/shard_map/pallas_call | solution.py:141
  154.3 2.1 fusion.73
  157.4 1.9 fusion.72
  159.9 2.3 multiply_add_fusion.1
  162.2 2.5 %shard_map.112 = (f32[768,128]{1,0:T(8,128)S(1)}, f32[768,128]{1,0:T(8,128)S(1)}, bf16[768,128]{1,0:T(8,128)(2,1)}, bf16[768,128]{1,0:T(8,128)(2,1)S(1)}) custom-call(f32[3,768,128]{2,1,0:T(8,128)S(1)} %get-tuple-element.206.d_ref, bf16[1536,1536]{1,0:T(8,128)(2,1)S(1)} %bitcast.133), custom_call_target="tpu_custom_call" | custom-call | flops 1207959552 | bytes 4718592 | tf_op jit(solution)/shard_map/pallas_call | solution.py:253
  165.5 2.3 shard_map.111
  171.8 12.6 %shard_map.113 = (bf16[8,2,16,128]{3,2,1,0:T(8,128)(2,1)}, bf16[768,128]{1,0:T(8,128)(2,1)}, bf16[768,128]{1,0:T(8,128)(2,1)}) custom-call(f32[2,16,128]{2,1,0:T(8,128)} %slice_add_fusion.19.part_ref, f32[2,16,128]{2,1,0:T(8,128)} %slice_add_fusion.18.share_ref, bf16[768,128]{1,0:T(8,128)(2,1)} %copy-done.8, bf16[768,128]{1,0:T(8,128)(2,1)} %copy-done.11), custom_call_target="tpu_custom_call" | custom-call | tf_op jit(solution)/shard_map/pallas_call | solution.py:141
  184.4 2.1 fusion.71
  187.5 1.9 fusion.70
  190.0 3.3 %multiply_add_fusion = (f32[3,768,128]{2,1,0:T(8,128)S(1)}, f32[3,768,128]{2,1,0:T(8,128)}) fusion(f32[3,768,128]{2,1,0:T(8,128)S(1)} %get-tuple-element.206.d_ref, f32[3,768,128]{2,1,0:T(8,128)} %copy-done.16, f32[3,768,128]{2,1,0:T(8,128)} %fusion.70, f32[3,768,256]{2,1,0:T(8,128)S(1)} %fusion.95, f32[3,768]{1,0:T(4,128)S(1)} %fusion.116), kind=kLoop, calls=%fused_computation.70 | loop fusion | flops 2064384 | bytes 8266752 | tf_op jit(solution)/shard_map/add | solution.py:385
  193.4 2.3 shard_map.115
  196.4 2.3 shard_map.114
  203.0 12.9 %shard_map.116 = (bf16[8,2,16,128]{3,2,1,0:T(8,128)(2,1)}, bf16[768,128]{1,0:T(8,128)(2,1)}, bf16[768,128]{1,0:T(8,128)(2,1)}) custom-call(f32[2,16,128]{2,1,0:T(8,128)} %slice_add_fusion.17.part_ref, f32[2,16,128]{2,1,0:T(8,128)} %slice_add_fusion.16.share_ref, bf16[768,128]{1,0:T(8,128)(2,1)} %copy-done.4, bf16[768,128]{1,0:T(8,128)(2,1)} %copy-done.5), custom_call_target="tpu_custom_call" | custom-call | tf_op jit(solution)/shard_map/pallas_call | solution.py:141
  221.8 9.6 %shard_map.117 = f32[32,8,128]{2,1,0:T(8,128)} custom-call(f32[8,128]{1,0:T(8,128)} %select_maximum_fusion.x_ref), custom_call_target="tpu_custom_call" | custom-call | tf_op jit(solution)/shard_map/pallas_call | solution.py:72
  (214 shorter events, 45.9 us)
Async XLA Ops:
  0.6 7.7 %copy-start = (bf16[2,16,1536]{2,1,0:T(8,128)(2,1)S(1)}, bf16[2,16,1536]{2,1,0:T(8,128)(2,1)}, u32[]{:S(2)}) copy-start(bf16[2,16,1536]{2,1,0:T(8,128)(2,1)} %param.26) | copy-start | bytes 294916
  2.2 72.9 %collective-permute-start.1 = (s32[9]{0:T(128)S(1)}, s32[9]{0:T(128)S(1)}, u32[]{:S(2)}, u32[]{:S(2)}) collective-permute-start(s32[9]{0:T(128)S(1)} %get-tuple-element.267), channel_id=1, source_target_pairs={{28,0},{0,4},{4,8},{8,12},{12,16},{16,20},{20,24},{24,28},{29,1},{... | collective-permute-start | bytes 116 | tf_op jit(solution)/shard_map/ppermute | solution.py:23
  5.2 9.7 %copy-start.25 = (s32[2,1536]{1,0:T(2,128)S(1)}, s32[2,1536]{1,0:T(2,128)}, u32[]{:S(2)}) copy-start(s32[2,1536]{1,0:T(2,128)} %param.29) | copy-start | bytes 36868
  5.2 71.3 %collective-permute-start.4 = (s32[9]{0:T(128)S(1)}, s32[9]{0:T(128)S(1)}, u32[]{:S(2)}, u32[]{:S(2)}) collective-permute-start(s32[9]{0:T(128)S(1)} %get-tuple-element.268), channel_id=1, source_target_pairs={{4,0},{8,4},{12,8},{16,12},{20,16},{24,20},{28,24},{0,28},{5,1},{9... | collective-permute-start | bytes 116 | tf_op jit(solution)/shard_map/ppermute | solution.py:23
  12.8 71.4 %collective-permute-start.3 = (bf16[16,1536]{1,0:T(8,128)(2,1)S(1)}, bf16[16,1536]{1,0:T(8,128)(2,1)S(1)}, u32[]{:S(2)}, u32[]{:S(2)}) collective-permute-start(bf16[16,1536]{1,0:T(8,128)(2,1)S(1)} %get-tuple-element.241), channel_id=1, source_target_pairs={{4,0},{8,4},{12,8},{16,12},{20,16},{24,20},{28,24},{0,28},{5,1},{9... | collective-permute-start | bytes 147464 | tf_op jit(solution)/shard_map/ppermute | solution.py:23
  44.7 29.8 %copy-start.27 = (s32[2]{0:T(128)S(1)}, s32[2]{0:T(128)}, u32[]{:S(2)}) copy-start(s32[2]{0:T(128)} %param.30) | copy-start | bytes 28
  44.7 29.9 %copy-start.24 = (f32[2,8,16,16]{3,2,1,0:T(8,128)S(1)}, f32[2,8,16,16]{3,2,1,0:T(8,128)}, u32[]{:S(2)}) copy-start(f32[2,8,16,16]{3,2,1,0:T(8,128)} %param.27) | copy-start | bytes 49156
  44.7 32.2 %collective-permute-start.8 = (f32[768]{0:T(1024)S(1)}, f32[768]{0:T(1024)S(1)}, u32[]{:S(2)}, u32[]{:S(2)}) collective-permute-start(f32[768]{0:T(1024)S(1)} %get-tuple-element.194), channel_id=1, source_target_pairs={{4,0},{8,4},{12,8},{16,12},{20,16},{24,20},{28,24},{0,28},{5,1},{9... | collective-permute-start | bytes 9224 | tf_op jit(solution)/shard_map/ppermute | solution.py:23
  73.9 7.5 %collective-permute-start.7 = (f32[768]{0:T(1024)S(1)}, f32[768]{0:T(1024)S(1)}, u32[]{:S(2)}, u32[]{:S(2)}) collective-permute-start(f32[768]{0:T(1024)S(1)} %get-tuple-element.193), channel_id=1, source_target_pairs={{28,0},{0,4},{4,8},{8,12},{12,16},{16,20},{20,24},{24,28},{29,1},{... | collective-permute-start | bytes 9224 | tf_op jit(solution)/shard_map/ppermute | solution.py:23
  75.1 9.2 %collective-permute-start.2 = (bf16[16,1536]{1,0:T(8,128)(2,1)S(1)}, bf16[16,1536]{1,0:T(8,128)(2,1)S(1)}, u32[]{:S(2)}, u32[]{:S(2)}) collective-permute-start(bf16[16,1536]{1,0:T(8,128)(2,1)S(1)} %get-tuple-element.242), channel_id=1, source_target_pairs={{28,0},{0,4},{4,8},{8,12},{12,16},{16,20},{20,24},{24,28},{29,1},{... | collective-permute-start | bytes 147464 | tf_op jit(solution)/shard_map/ppermute | solution.py:23
  76.5 7.0 %collective-permute-start.5 = (f32[8,16,16]{2,0,1:T(8,128)S(1)}, f32[8,16,16]{2,0,1:T(8,128)S(1)}, u32[]{:S(2)}, u32[]{:S(2)}) collective-permute-start(f32[8,16,16]{2,0,1:T(8,128)S(1)} %get-tuple-element.239), channel_id=1, source_target_pairs={{28,0},{0,4},{4,8},{8,12},{12,16},{16,20},{20,24},{24,28},{29,1},{... | collective-permute-start | bytes 24584 | tf_op jit(solution)/shard_map/ppermute | solution.py:23
  76.9 6.6 %collective-permute-start.6 = (f32[8,16,16]{2,0,1:T(8,128)S(1)}, f32[8,16,16]{2,0,1:T(8,128)S(1)}, u32[]{:S(2)}, u32[]{:S(2)}) collective-permute-start(f32[8,16,16]{2,0,1:T(8,128)S(1)} %get-tuple-element.240), channel_id=1, source_target_pairs={{4,0},{8,4},{12,8},{16,12},{20,16},{24,20},{28,24},{0,28},{5,1},{9... | collective-permute-start | bytes 24584 | tf_op jit(solution)/shard_map/ppermute | solution.py:23
  81.4 11.6 %collective-permute-start = (f32[768,128]{1,0:T(8,128)S(1)}, f32[768,128]{1,0:T(8,128)S(1)}, u32[]{:S(2)}, u32[]{:S(2)}) collective-permute-start(f32[768,128]{1,0:T(8,128)S(1)} %slice_bitcast_fusion), channel_id=1, source_target_pairs={{28,0},{0,4},{4,8},{8,12},{12,16},{16,20},{20,24},{24,28},{29,1},{... | collective-permute-start | bytes 1179656 | tf_op jit(solution)/shard_map/ppermute | solution.py:23
  93.3 10.8 %slice-start = ((s8[4718592]{0:T(1024)(128)(4,1)}), s8[524288]{0:T(1024)(128)(4,1)S(1)}, s32[]{:S(2)}) async-start(s8[4718592]{0:T(1024)(128)(4,1)} %bitcast.120), calls=%async_computation | async-start | bytes 1048576
  103.1 5.9 %slice-start.8 = ((s8[4718592]{0:T(1024)(128)(4,1)}), s8[4194304]{0:T(1024)(128)(4,1)S(1)}, s32[]{:S(2)}) async-start(s8[4718592]{0:T(1024)(128)(4,1)} %bitcast.128), calls=%async_computation.8 | async-start | bytes 8388608
  103.6 5.4 %slice-start.9 = ((s8[4718592]{0:T(1024)(128)(4,1)}), s8[524288]{0:T(1024)(128)(4,1)S(1)}, s32[]{:S(2)}) async-start(s8[4718592]{0:T(1024)(128)(4,1)} %bitcast.128), calls=%async_computation.9 | async-start | bytes 1048576
  104.0 5.0 %copy-start.2 = (f32[3,768,128]{2,1,0:T(8,128)}, f32[3,768,128]{2,1,0:T(8,128)S(1)}, u32[]{:S(2)}) copy-start(f32[3,768,128]{2,1,0:T(8,128)S(1)} %get-tuple-element.216.d_ref) | copy-start | bytes 3538948
  104.0 9.0 %copy-start.14 = (f32[3,768,128]{2,1,0:T(8,128)}, f32[3,768,128]{2,1,0:T(8,128)S(1)}, u32[]{:S(2)}) copy-start(f32[3,768,128]{2,1,0:T(8,128)S(1)} %get-tuple-element.217) | copy-start | bytes 3538948
  113.8 17.4 %slice-start.10 = ((s8[4718592]{0:T(1024)(128)(4,1)}), s8[524288]{0:T(1024)(128)(4,1)S(1)}, s32[]{:S(2)}) async-start(s8[4718592]{0:T(1024)(128)(4,1)} %bitcast.130), calls=%async_computation.10 | async-start | bytes 1048576
  130.1 4.9 %slice-start.2 = ((s8[4718592]{0:T(1024)(128)(4,1)}), s8[4194304]{0:T(1024)(128)(4,1)S(1)}, s32[]{:S(2)}) async-start(s8[4718592]{0:T(1024)(128)(4,1)} %bitcast.122), calls=%async_computation.2 | async-start | bytes 8388608
  130.7 4.4 %slice-start.3 = ((s8[4718592]{0:T(1024)(128)(4,1)}), s8[524288]{0:T(1024)(128)(4,1)S(1)}, s32[]{:S(2)}) async-start(s8[4718592]{0:T(1024)(128)(4,1)} %bitcast.122), calls=%async_computation.3 | async-start | bytes 1048576
  131.2 6.2 %copy-start.17 = (f32[3,768,128]{2,1,0:T(8,128)}, f32[3,768,128]{2,1,0:T(8,128)S(1)}, u32[]{:S(2)}) copy-start(f32[3,768,128]{2,1,0:T(8,128)S(1)} %get-tuple-element.211) | copy-start | bytes 3538948
  139.0 23.2 %slice-start.12 = ((s8[4718592]{0:T(1024)(128)(4,1)}), s8[524288]{0:T(1024)(128)(4,1)S(1)}, s32[]{:S(2)}) async-start(s8[4718592]{0:T(1024)(128)(4,1)} %bitcast.132), calls=%async_computation.12 | async-start | bytes 1048576
  154.3 8.0 %slice-start.13 = ((s8[4718592]{0:T(1024)(128)(4,1)}), s8[4194304]{0:T(1024)(128)(4,1)S(1)}, s32[]{:S(2)}) async-start(s8[4718592]{0:T(1024)(128)(4,1)} %bitcast.132), calls=%async_computation.13 | async-start | bytes 8388608
  159.4 6.1 %slice-start.4 = ((s8[4718592]{0:T(1024)(128)(4,1)}), s8[4194304]{0:T(1024)(128)(4,1)S(1)}, s32[]{:S(2)}) async-start(s8[4718592]{0:T(1024)(128)(4,1)} %bitcast.124), calls=%async_computation.4 | async-start | bytes 8388608
  159.9 5.5 %slice-start.5 = ((s8[4718592]{0:T(1024)(128)(4,1)}), s8[524288]{0:T(1024)(128)(4,1)S(1)}, s32[]{:S(2)}) async-start(s8[4718592]{0:T(1024)(128)(4,1)} %bitcast.124), calls=%async_computation.5 | async-start | bytes 1048576
  162.2 5.6 %copy-start.16 = (f32[3,768,128]{2,1,0:T(8,128)}, f32[3,768,128]{2,1,0:T(8,128)S(1)}, u32[]{:S(2)}) copy-start(f32[3,768,128]{2,1,0:T(8,128)S(1)} %get-tuple-element.207) | copy-start | bytes 3538948
  169.4 23.9 %slice-start.14 = ((s8[4718592]{0:T(1024)(128)(4,1)}), s8[524288]{0:T(1024)(128)(4,1)S(1)}, s32[]{:S(2)}) async-start(s8[4718592]{0:T(1024)(128)(4,1)} %bitcast.134), calls=%async_computation.14 | async-start | bytes 1048576
  184.4 9.0 %slice-start.15 = ((s8[4718592]{0:T(1024)(128)(4,1)}), s8[4194304]{0:T(1024)(128)(4,1)S(1)}, s32[]{:S(2)}) async-start(s8[4718592]{0:T(1024)(128)(4,1)} %bitcast.134), calls=%async_computation.15 | async-start | bytes 8388608
  189.5 6.9 %slice-start.6 = ((s8[4718592]{0:T(1024)(128)(4,1)}), s8[4194304]{0:T(1024)(128)(4,1)S(1)}, s32[]{:S(2)}) async-start(s8[4718592]{0:T(1024)(128)(4,1)} %bitcast.126), calls=%async_computation.6 | async-start | bytes 8388608
  190.0 6.4 %slice-start.7 = ((s8[4718592]{0:T(1024)(128)(4,1)}), s8[524288]{0:T(1024)(128)(4,1)S(1)}, s32[]{:S(2)}) async-start(s8[4718592]{0:T(1024)(128)(4,1)} %bitcast.126), calls=%async_computation.7 | async-start | bytes 1048576
  219.7 13.8 %copy-start.1 = (bf16[2,16,1536]{2,1,0:T(8,128)(2,1)S(1)}, bf16[2,16,1536]{2,1,0:T(8,128)(2,1)}, u32[]{:S(2)}) copy-start(bf16[2,16,1536]{2,1,0:T(8,128)(2,1)} %param.26) | copy-start | bytes 294916
  (21 other events, 31.8 us)

commit v4 on v3

--- a/solution.py
+++ b/solution.py
@@ -376,8 +376,10 @@
             jnp.einsum("sjn,snc->sjc", share_modes, split(ends, 2), preferred_element_type=f32)
         )
         everyone, rim_up, rim_low = exchange(fit(mapped), share, up_low, low_low, 3)
-        mapped = mapped.at[0].add(rim_up.astype(f32) * live[0])
-        mapped = mapped.at[-1].add(-rim_low.astype(f32) * live[-1])
+        before = [rim_up.astype(f32)] + uppers
+        after = lowers + [rim_low.astype(f32)]
+        rest = jnp.stack([u - l for u, l in zip(before, after)])
+        mapped = (diagonal * direction + rest) * live
         residual = residual - (mapped - correction_of(everyone))
         sums.append(jnp.sum(residual[1:] * residual[1:], axis=(0, 1)))
         if turn_index + 1 < STEPS:

time: 234 us -> 236 us (level)
  local copies, waits for them, and re-layouts: 15.4 us -> 19.7 us
  Pallas kernels: 139 us -> 143 us
  other arithmetic: 35.2 us -> 32 us
  matrix products: 15.1 us -> 12.5 us
    scatter-add x8 -> x0, other arithmetic: 10.8 us -> none  [the longest x4 6.54 us: shards(): mapped = mapped.at[0].add(rim_up.astype(f32) * live[0])]
    another operation x0 -> x8, other arithmetic: none -> 7.84 us  [shards(): rest = jnp.stack([u - l for u, l in zip(before, after)])]
    pallas_call x4, Pallas kernels: 50.9 us -> 54.5 us  [exchange(): pl.pallas_call(functools.partial(exchange_kernel, count), out_shape=[jax....]
    unnamed x89 -> x145, local copies, waits for them, and re-layouts: 8.25 us -> 11.3 us
    dot_general x5, matrix products: 5.13 us -> 2.56 us  [correction_of(): amounts = jnp.dot(coarse, everyone.astype(f32), precision=highest)]
  transfers between devices with their start and end apart: 9 -> 9, of which waited for: 2 -> 3; matrix products, arithmetic and copies ran while one was open for 5% -> 6% of each run, Pallas kernels for 22% -> 22%
where the time goes in v4:
time: 236 us; the launch traced here: 235 us
  Pallas kernels  143 us (61%)
  other arithmetic  32 us (14%)
  local copies, waits for them, and re-layouts  19.7 us (8%)
  starting transfers between devices  16 us (7%)
  matrix products  12.5 us (5%)
  waiting for transfers between devices  9.55 us (4%)
    pallas_call x4, Pallas kernels, exchange(): pl.pallas_call(functools.partial(exchange_kernel, count), out_shape=[jax....  54.5 us
    pallas_call x2, Pallas kernels, slot_operator(): pl.pallas_call(setup_kernel, grid=(1, size // depth), out_shape=[jax.Shap...  52.4 us
    pallas_call x8, Pallas kernels, apply_operator(): pl.pallas_call(functools.partial(apply_kernel, sub), grid=(2,), out_shape...  18.5 us
    pallas_call x2, Pallas kernels, push_gather(): pl.pallas_call(functools.partial(gather_kernel, axes, sizes), out_shape=j...  17.9 us
    ppermute x9, starting transfers between devices, from_behind(): return lax.ppermute(block, axis, route)  16 us
    unnamed x145, local copies, waits for them, and re-layouts  11.3 us
    ppermute x9, waiting for transfers between devices, from_behind(): return lax.ppermute(block, axis, route)  9.55 us
    another operation x8, other arithmetic, shards(): rest = jnp.stack([u - l for u, l in zip(before, after)])  7.84 us
  transfers between devices with their start and end apart: 9, of which 3 were waited for; matrix products, arithmetic and copies ran while one was open for 6% of the time, Pallas kernels for 22%

profile of v4, /device:TPU:0, one launch (start us, length us, event | category | flops | bytes accessed | tf_op | source)
XLA Modules:
  0.0 234.9 jit_solution(2129367287366261346)
XLA Ops:
  2.2 3.0 %collective-permute-start.1 = (s32[9]{0:T(128)S(1)}, s32[9]{0:T(128)S(1)}, u32[]{:S(2)}, u32[]{:S(2)}) collective-permute-start(s32[9]{0:T(128)S(1)} %get-tuple-element.171), channel_id=1, source_target_pairs={{28,0},{0,4},{4,8},{8,12},{12,16},{16,20},{20,24},{24,28},{29,1},{... | collective-permute-start | bytes 116 | tf_op jit(solution)/shard_map/ppermute | solution.py:23
  5.2 3.1 %collective-permute-start.4 = (s32[9]{0:T(128)S(1)}, s32[9]{0:T(128)S(1)}, u32[]{:S(2)}, u32[]{:S(2)}) collective-permute-start(s32[9]{0:T(128)S(1)} %get-tuple-element.172), channel_id=1, source_target_pairs={{4,0},{8,4},{12,8},{16,12},{20,16},{24,20},{28,24},{0,28},{5,1},{9... | collective-permute-start | bytes 116 | tf_op jit(solution)/shard_map/ppermute | solution.py:23
  8.3 4.5 %fusion.3 = bf16[2,16,1536]{2,1,0:T(8,128)(2,1)S(1)} fusion(bf16[2,16,1536]{2,1,0:T(8,128)(2,1)S(1)} %copy-done, s32[2,1536]{1,0:T(2,128)} %param.13), kind=kOutput, calls=%fused_computation.4 | convolution fusion | flops 155762688 | bytes 208896 | tf_op jit(solution)/shard_map/sjn,skn->sjk/dot_general | solution.py:300
  12.8 2.0 collective-permute-start.3
  15.4 1.7 copy.19.col_ref
  17.1 26.2 %shard_map.104 = (bf16[1536,1536]{1,0:T(8,128)(2,1)}, f32[1536,1]{1,0:T(8,128)}) custom-call(s32[2,1,1536]{2,1,0:T(1,128)} %broadcast_in_dim.45.row_ref, s32[2,1536,1]{2,1,0:T(8,128)} %copy.19.col_ref, f32[2,1536,1536]{2,1,0:T(8,128)} %a_ref.3), custom_call_target="tpu_custom_call" | custom-call | flops 14495514624 | bytes 14155776 | tf_op jit(solution)/shard_map/pallas_call | solution.py:198
  43.3 1.4 slice_reduce_fusion.1
  44.7 1.5 collective-permute-start.8
  46.2 26.2 %shard_map.103 = (bf16[1536,1536]{1,0:T(8,128)(2,1)}, f32[1536,1]{1,0:T(8,128)}) custom-call(s32[2,1,1536]{2,1,0:T(1,128)} %broadcast_in_dim.45.row_ref, s32[2,1536,1]{2,1,0:T(8,128)} %copy.19.col_ref, f32[2,1536,1536]{2,1,0:T(8,128)} %a_ref.3), custom_call_target="tpu_custom_call" | custom-call | flops 14495514624 | bytes 14155776 | tf_op jit(solution)/shard_map/pallas_call | solution.py:198
  72.4 1.5 slice_reduce_fusion
  78.0 4.5 %collective-permute-start.6 = (f32[8,16,16]{2,0,1:T(8,128)S(1)}, f32[8,16,16]{2,0,1:T(8,128)S(1)}, u32[]{:S(2)}, u32[]{:S(2)}) collective-permute-start(f32[8,16,16]{2,0,1:T(8,128)S(1)} %get-tuple-element.144), channel_id=1, source_target_pairs={{4,0},{8,4},{12,8},{16,12},{20,16},{24,20},{28,24},{0,28},{5,1},{9... | collective-permute-start | bytes 24584 | tf_op jit(solution)/shard_map/ppermute | solution.py:23
  82.5 1.5 collective-permute-done.5
  86.4 7.7 %collective-permute-done = f32[768,128]{1,0:T(8,128)S(1)} collective-permute-done((f32[768,128]{1,0:T(8,128)S(1)}, f32[768,128]{1,0:T(8,128)S(1)}, u32[]{:S(2)}, u32[]{:S(2)}) %collective-permute-start) | collective-permute-done | bytes 393248 | tf_op jit(solution)/shard_map/ppermute | solution.py:23
  95.3 7.9 %shard_map.102 = bf16[8,2,16,128]{3,2,1,0:T(8,128)(2,1)} custom-call(bf16[2,16,128]{2,1,0:T(8,128)(2,1)} %fusion.122.x_ref), custom_call_target="tpu_custom_call" | custom-call | tf_op jit(solution)/shard_map/pallas_call | solution.py:72
  105.2 2.0 slice-done.1
  107.3 2.3 shard_map.105
  110.2 2.3 shard_map.106
  117.6 13.5 %shard_map.107 = (bf16[8,2,16,128]{3,2,1,0:T(8,128)(2,1)}, bf16[768,128]{1,0:T(8,128)(2,1)}, bf16[768,128]{1,0:T(8,128)(2,1)}) custom-call(f32[2,16,128]{2,1,0:T(8,128)} %slice_add_fusion.16.part_ref, f32[2,16,128]{2,1,0:T(8,128)} %slice_add_fusion.15.share_ref, bf16[768,128]{1,0:T(8,128)(2,1)} %copy-done.10, bf16[768,128]{1,0:T(8,128)(2,1)} %copy-done.7), custom_call_target="tpu_custom_call" | custom-call | tf_op jit(solution)/shard_map/pallas_call | solution.py:141
  132.2 1.2 subtract_bitcast_fusion.12
  134.2 2.2 multiply_add_fusion.2
  136.4 2.3 shard_map.109
  139.4 2.3 shard_map.108
  146.3 14.0 %shard_map.110 = (bf16[8,2,16,128]{3,2,1,0:T(8,128)(2,1)}, bf16[768,128]{1,0:T(8,128)(2,1)}, bf16[768,128]{1,0:T(8,128)(2,1)}) custom-call(f32[2,16,128]{2,1,0:T(8,128)} %slice_add_fusion.14.part_ref, f32[2,16,128]{2,1,0:T(8,128)} %slice_add_fusion.13.share_ref, bf16[768,128]{1,0:T(8,128)(2,1)} %copy-done.8, bf16[768,128]{1,0:T(8,128)(2,1)} %copy-done.11), custom_call_target="tpu_custom_call" | custom-call | tf_op jit(solution)/shard_map/pallas_call | solution.py:141
  164.1 2.3 shard_map.112
  167.1 2.3 shard_map.111
  174.0 13.0 %shard_map.113 = (bf16[8,2,16,128]{3,2,1,0:T(8,128)(2,1)}, bf16[768,128]{1,0:T(8,128)(2,1)}, bf16[768,128]{1,0:T(8,128)(2,1)}) custom-call(f32[2,16,128]{2,1,0:T(8,128)} %slice_add_fusion.12.part_ref, f32[2,16,128]{2,1,0:T(8,128)} %slice_add_fusion.11.share_ref, bf16[768,128]{1,0:T(8,128)(2,1)} %copy-done.9, bf16[768,128]{1,0:T(8,128)(2,1)} %copy-done.12), custom_call_target="tpu_custom_call" | custom-call | tf_op jit(solution)/shard_map/pallas_call | solution.py:141
  190.2 1.7 multiply_add_fusion
  191.9 2.3 shard_map.115
  194.8 2.3 shard_map.114
  202.9 14.0 %shard_map.116 = (bf16[8,2,16,128]{3,2,1,0:T(8,128)(2,1)}, bf16[768,128]{1,0:T(8,128)(2,1)}, bf16[768,128]{1,0:T(8,128)(2,1)}) custom-call(f32[2,16,128]{2,1,0:T(8,128)} %slice_add_fusion.10.part_ref, f32[2,16,128]{2,1,0:T(8,128)} %slice_add_fusion.9.share_ref, bf16[768,128]{1,0:T(8,128)(2,1)} %copy-done.5, bf16[768,128]{1,0:T(8,128)(2,1)} %copy-done.6), custom_call_target="tpu_custom_call" | custom-call | tf_op jit(solution)/shard_map/pallas_call | solution.py:141
  220.9 1.3 multiply_reduce_fusion
  222.7 10.0 %shard_map.117 = f32[32,8,128]{2,1,0:T(8,128)} custom-call(f32[8,128]{1,0:T(8,128)} %select_maximum_fusion.x_ref), custom_call_target="tpu_custom_call" | custom-call | tf_op jit(solution)/shard_map/pallas_call | solution.py:72
  (267 shorter events, 49.2 us)
Async XLA Ops:
  0.6 7.7 %copy-start = (bf16[2,16,1536]{2,1,0:T(8,128)(2,1)S(1)}, bf16[2,16,1536]{2,1,0:T(8,128)(2,1)}, u32[]{:S(2)}) copy-start(bf16[2,16,1536]{2,1,0:T(8,128)(2,1)} %param.10) | copy-start | bytes 294916
  2.2 72.9 %collective-permute-start.1 = (s32[9]{0:T(128)S(1)}, s32[9]{0:T(128)S(1)}, u32[]{:S(2)}, u32[]{:S(2)}) collective-permute-start(s32[9]{0:T(128)S(1)} %get-tuple-element.171), channel_id=1, source_target_pairs={{28,0},{0,4},{4,8},{8,12},{12,16},{16,20},{20,24},{24,28},{29,1},{... | collective-permute-start | bytes 116 | tf_op jit(solution)/shard_map/ppermute | solution.py:23
  5.2 9.7 %copy-start.34 = (s32[2,1536]{1,0:T(2,128)S(1)}, s32[2,1536]{1,0:T(2,128)}, u32[]{:S(2)}) copy-start(s32[2,1536]{1,0:T(2,128)} %param.13) | copy-start | bytes 36868
  5.2 71.9 %collective-permute-start.4 = (s32[9]{0:T(128)S(1)}, s32[9]{0:T(128)S(1)}, u32[]{:S(2)}, u32[]{:S(2)}) collective-permute-start(s32[9]{0:T(128)S(1)} %get-tuple-element.172), channel_id=1, source_target_pairs={{4,0},{8,4},{12,8},{16,12},{20,16},{24,20},{28,24},{0,28},{5,1},{9... | collective-permute-start | bytes 116 | tf_op jit(solution)/shard_map/ppermute | solution.py:23
  12.8 72.3 %collective-permute-start.3 = (bf16[16,1536]{1,0:T(8,128)(2,1)S(1)}, bf16[16,1536]{1,0:T(8,128)(2,1)S(1)}, u32[]{:S(2)}, u32[]{:S(2)}) collective-permute-start(bf16[16,1536]{1,0:T(8,128)(2,1)S(1)} %get-tuple-element.145), channel_id=1, source_target_pairs={{4,0},{8,4},{12,8},{16,12},{20,16},{24,20},{28,24},{0,28},{5,1},{9... | collective-permute-start | bytes 147464 | tf_op jit(solution)/shard_map/ppermute | solution.py:23
  44.7 29.8 %copy-start.55 = (s32[2]{0:T(128)S(1)}, s32[2]{0:T(128)}, u32[]{:S(2)}) copy-start(s32[2]{0:T(128)} %param.14) | copy-start | bytes 28
  44.7 29.9 %copy-start.28 = (f32[2,8,16,16]{3,2,1,0:T(8,128)S(1)}, f32[2,8,16,16]{3,2,1,0:T(8,128)}, u32[]{:S(2)}) copy-start(f32[2,8,16,16]{3,2,1,0:T(8,128)} %param.11) | copy-start | bytes 49156
  44.7 33.3 %collective-permute-start.8 = (f32[768]{0:T(1024)S(1)}, f32[768]{0:T(1024)S(1)}, u32[]{:S(2)}, u32[]{:S(2)}) collective-permute-start(f32[768]{0:T(1024)S(1)} %get-tuple-element.98), channel_id=1, source_target_pairs={{4,0},{8,4},{12,8},{16,12},{20,16},{24,20},{28,24},{0,28},{5,1},{9... | collective-permute-start | bytes 9224 | tf_op jit(solution)/shard_map/ppermute | solution.py:23
  73.9 8.6 %collective-permute-start.7 = (f32[768]{0:T(1024)S(1)}, f32[768]{0:T(1024)S(1)}, u32[]{:S(2)}, u32[]{:S(2)}) collective-permute-start(f32[768]{0:T(1024)S(1)} %get-tuple-element.97), channel_id=1, source_target_pairs={{28,0},{0,4},{4,8},{8,12},{12,16},{16,20},{20,24},{24,28},{29,1},{... | collective-permute-start | bytes 9224 | tf_op jit(solution)/shard_map/ppermute | solution.py:23
  74.6 19.8 %copy-start.35 = (bf16[2,16,768]{2,1,0:T(8,128)(2,1)}, bf16[2,16,768]{2,1,0:T(8,128)(2,1)S(1)}, u32[]{:S(2)}) copy-start(bf16[2,16,768]{2,1,0:T(8,128)(2,1)S(1)} %get-tuple-element.147) | copy-start | bytes 147460
  74.6 19.8 %copy-start.40 = (bf16[2,16,768]{2,1,0:T(8,128)(2,1)}, bf16[2,16,768]{2,1,0:T(8,128)(2,1)S(1)}, u32[]{:S(2)}) copy-start(bf16[2,16,768]{2,1,0:T(8,128)(2,1)S(1)} %get-tuple-element.148) | copy-start | bytes 147460
  75.1 10.6 %collective-permute-start.2 = (bf16[16,1536]{1,0:T(8,128)(2,1)S(1)}, bf16[16,1536]{1,0:T(8,128)(2,1)S(1)}, u32[]{:S(2)}, u32[]{:S(2)}) collective-permute-start(bf16[16,1536]{1,0:T(8,128)(2,1)S(1)} %get-tuple-element.146), channel_id=1, source_target_pairs={{28,0},{0,4},{4,8},{8,12},{12,16},{16,20},{20,24},{24,28},{29,1},{... | collective-permute-start | bytes 147464 | tf_op jit(solution)/shard_map/ppermute | solution.py:23
  77.1 7.0 %collective-permute-start.5 = (f32[8,16,16]{2,0,1:T(8,128)S(1)}, f32[8,16,16]{2,0,1:T(8,128)S(1)}, u32[]{:S(2)}, u32[]{:S(2)}) collective-permute-start(f32[8,16,16]{2,0,1:T(8,128)S(1)} %get-tuple-element.143), channel_id=1, source_target_pairs={{28,0},{0,4},{4,8},{8,12},{12,16},{16,20},{20,24},{24,28},{29,1},{... | collective-permute-start | bytes 24584 | tf_op jit(solution)/shard_map/ppermute | solution.py:23
  78.0 6.4 %collective-permute-start.6 = (f32[8,16,16]{2,0,1:T(8,128)S(1)}, f32[8,16,16]{2,0,1:T(8,128)S(1)}, u32[]{:S(2)}, u32[]{:S(2)}) collective-permute-start(f32[8,16,16]{2,0,1:T(8,128)S(1)} %get-tuple-element.144), channel_id=1, source_target_pairs={{4,0},{8,4},{12,8},{16,12},{20,16},{24,20},{28,24},{0,28},{5,1},{9... | collective-permute-start | bytes 24584 | tf_op jit(solution)/shard_map/ppermute | solution.py:23
  82.5 11.6 %collective-permute-start = (f32[768,128]{1,0:T(8,128)S(1)}, f32[768,128]{1,0:T(8,128)S(1)}, u32[]{:S(2)}, u32[]{:S(2)}) collective-permute-start(f32[768,128]{1,0:T(8,128)S(1)} %slice_bitcast_fusion), channel_id=1, source_target_pairs={{28,0},{0,4},{4,8},{8,12},{12,16},{16,20},{20,24},{24,28},{29,1},{... | collective-permute-start | bytes 1179656 | tf_op jit(solution)/shard_map/ppermute | solution.py:23
  85.8 18.5 %copy-start.21 = (bf16[16,1536]{1,0:T(8,128)(2,1)}, bf16[16,1536]{1,0:T(8,128)(2,1)S(1)}, u32[]{:S(2)}) copy-start(bf16[16,1536]{1,0:T(8,128)(2,1)S(1)} %collective-permute-done.2) | copy-start | bytes 147460
  94.4 10.8 %slice-start = ((s8[4718592]{0:T(1024)(128)(4,1)}), s8[524288]{0:T(1024)(128)(4,1)S(1)}, s32[]{:S(2)}) async-start(s8[4718592]{0:T(1024)(128)(4,1)} %bitcast.120), calls=%async_computation | async-start | bytes 1048576
  104.3 5.9 %slice-start.8 = ((s8[4718592]{0:T(1024)(128)(4,1)}), s8[4194304]{0:T(1024)(128)(4,1)S(1)}, s32[]{:S(2)}) async-start(s8[4718592]{0:T(1024)(128)(4,1)} %bitcast.128), calls=%async_computation.8 | async-start | bytes 8388608
  104.8 5.4 %slice-start.9 = ((s8[4718592]{0:T(1024)(128)(4,1)}), s8[524288]{0:T(1024)(128)(4,1)S(1)}, s32[]{:S(2)}) async-start(s8[4718592]{0:T(1024)(128)(4,1)} %bitcast.128), calls=%async_computation.9 | async-start | bytes 1048576
  105.2 5.0 %copy-start.2 = (f32[3,768,128]{2,1,0:T(8,128)}, f32[3,768,128]{2,1,0:T(8,128)S(1)}, u32[]{:S(2)}) copy-start(f32[3,768,128]{2,1,0:T(8,128)S(1)} %get-tuple-element.114.d_ref) | copy-start | bytes 3538948
  105.2 9.8 %copy-start.13 = (f32[3,768,128]{2,1,0:T(8,128)}, f32[3,768,128]{2,1,0:T(8,128)S(1)}, u32[]{:S(2)}) copy-start(f32[3,768,128]{2,1,0:T(8,128)S(1)} %get-tuple-element.115) | copy-start | bytes 3538948
  115.0 21.3 %slice-start.10 = ((s8[4718592]{0:T(1024)(128)(4,1)}), s8[524288]{0:T(1024)(128)(4,1)S(1)}, s32[]{:S(2)}) async-start(s8[4718592]{0:T(1024)(128)(4,1)} %bitcast.130), calls=%async_computation.10 | async-start | bytes 1048576
  131.0 5.3 %slice-start.11 = ((s8[4718592]{0:T(1024)(128)(4,1)}), s8[4194304]{0:T(1024)(128)(4,1)S(1)}, s32[]{:S(2)}) async-start(s8[4718592]{0:T(1024)(128)(4,1)} %bitcast.130), calls=%async_computation.11 | async-start | bytes 8388608
  133.6 5.7 %slice-start.2 = ((s8[4718592]{0:T(1024)(128)(4,1)}), s8[4194304]{0:T(1024)(128)(4,1)S(1)}, s32[]{:S(2)}) async-start(s8[4718592]{0:T(1024)(128)(4,1)} %bitcast.122), calls=%async_computation.2 | async-start | bytes 8388608
  134.1 5.2 %slice-start.3 = ((s8[4718592]{0:T(1024)(128)(4,1)}), s8[524288]{0:T(1024)(128)(4,1)S(1)}, s32[]{:S(2)}) async-start(s8[4718592]{0:T(1024)(128)(4,1)} %bitcast.122), calls=%async_computation.3 | async-start | bytes 1048576
  136.3 5.4 %copy-start.16 = (f32[3,768,128]{2,1,0:T(8,128)}, f32[3,768,128]{2,1,0:T(8,128)S(1)}, u32[]{:S(2)}) copy-start(f32[3,768,128]{2,1,0:T(8,128)S(1)} %get-tuple-element.111) | copy-start | bytes 3538948
  143.7 20.4 %slice-start.12 = ((s8[4718592]{0:T(1024)(128)(4,1)}), s8[524288]{0:T(1024)(128)(4,1)S(1)}, s32[]{:S(2)}) async-start(s8[4718592]{0:T(1024)(128)(4,1)} %bitcast.132), calls=%async_computation.12 | async-start | bytes 1048576
  164.1 5.3 %copy-start.14 = (f32[3,768,128]{2,1,0:T(8,128)}, f32[3,768,128]{2,1,0:T(8,128)S(1)}, u32[]{:S(2)}) copy-start(f32[3,768,128]{2,1,0:T(8,128)S(1)} %get-tuple-element.109) | copy-start | bytes 3538948
  171.4 20.4 %slice-start.14 = ((s8[4718592]{0:T(1024)(128)(4,1)}), s8[524288]{0:T(1024)(128)(4,1)S(1)}, s32[]{:S(2)}) async-start(s8[4718592]{0:T(1024)(128)(4,1)} %bitcast.134), calls=%async_computation.14 | async-start | bytes 1048576
  189.6 5.2 %slice-start.6 = ((s8[4718592]{0:T(1024)(128)(4,1)}), s8[4194304]{0:T(1024)(128)(4,1)S(1)}, s32[]{:S(2)}) async-start(s8[4718592]{0:T(1024)(128)(4,1)} %bitcast.126), calls=%async_computation.6 | async-start | bytes 8388608
  190.2 4.7 %slice-start.7 = ((s8[4718592]{0:T(1024)(128)(4,1)}), s8[524288]{0:T(1024)(128)(4,1)S(1)}, s32[]{:S(2)}) async-start(s8[4718592]{0:T(1024)(128)(4,1)} %bitcast.126), calls=%async_computation.7 | async-start | bytes 1048576
  220.9 14.1 %copy-start.1 = (bf16[2,16,1536]{2,1,0:T(8,128)(2,1)S(1)}, bf16[2,16,1536]{2,1,0:T(8,128)(2,1)}, u32[]{:S(2)}) copy-start(bf16[2,16,1536]{2,1,0:T(8,128)(2,1)} %param.10) | copy-start | bytes 294916
  (49 other events, 79.2 us)
